TPU v7x, 128 devices: a whole 4x4x4 slice. The times are simulated.
128 devices in a mesh: seq: 16 (over x, z), head: 8 (over y, core).
Axes of the slice: x: 4, y: 4, z: 4, core: 2. Of those that a mesh axis runs over, the one named last changes fastest.
Arguments:
- prompt_keys: bfloat16 [16384, 2048], P('seq', 'head'), may hold values from -6 to 6
- prompt_values: bfloat16 [16384, 4096], P('seq', 'head'), may hold values from -6 to 6
- prompt_input: float32 [8, 16384], P('head', 'seq'), may hold values from -3 to 0
- prompt_forget: float32 [8, 16384], P('head', 'seq'), may hold values from 0.4 to 17
- prompt_lengths: int32 [4], replicated, may hold values from 1 to 8192, 16384 in all
- response_prompt: int32 [32, 1], replicated, may hold values from 0 to 3
- resp_queries: bfloat16 [32, 512, 2048], P('seq', None, 'head'), may hold values from -6 to 6
- resp_keys: bfloat16 [32, 512, 2048], P('seq', None, 'head'), may hold values from -6 to 6
- resp_values: bfloat16 [32, 512, 4096], P('seq', None, 'head'), may hold values from -6 to 6
- resp_input: float32 [8, 32, 512], P('head', 'seq'), may hold values from -3 to 0
- resp_forget: float32 [8, 32, 512], P('head', 'seq'), may hold values from 0.4 to 17
- norm_gain: float32 [4096], P('head'), may hold values from 0.1 to 1.9
- out_grad: bfloat16 [32, 512, 4096], P('seq', None, 'head'), may hold values from -6 to 6
Outputs:
- resp_out: bfloat16 [32, 512, 4096], P('seq', None, 'head')
- prompt_key_grad: bfloat16 [16384, 2048], P('seq', 'head')
- prompt_value_grad: bfloat16 [16384, 4096], P('seq', 'head')
Inputs may be any that keep to these rules, and one draw needn't show every extreme that they name: `prompt_lengths`: prompt p covers the window positions from the sum of the earlier lengths onward; the lengths sum to 16384 and the longest is exactly half of 16384. `response_prompt`: every prompt is continued by at least one response.
All inputs are finite; a program needn't handle non-finite values.
Results may differ from a plain program's by a relative error of at most 0.025.
Values may be sent and summed in bfloat16 or wider, within the bound.
No kernel may reach another device: no remote copies, remote signals or barrier semaphores. Data moves between devices by JAX's collectives and lax.ppermute only.
A program may use at most 64 MiB of HBM per device.

v0:
```python
import math

import jax
import jax.numpy as jnp
from jax import lax
from jax.sharding import PartitionSpec as P


def copy_for_each(value, axis):
    length = lax.axis_size(axis)
    return lax.all_to_all(
        jnp.broadcast_to(value[None], (length, *value.shape)), axis, 0, 0, tiled=True
    )


def combined_pairwise(pieces, combine):
    while len(jax.tree.leaves(pieces)[0]) > 1:
        pieces = jax.vmap(combine)(*(pieces[side::2] for side in (0, 1)))
    return pieces[0]


def carried_in(value, axis, combine, identity):
    length, here = (lax.axis_size(axis), lax.axis_index(axis))
    passed = jnp.arange(length) > here

    def kept(part, zero, own):
        part = jnp.where(
            passed.reshape(-1, *(1 for _ in own.shape)), part, jnp.asarray(zero, own.dtype)
        )
        return part[::-1]

    pieces = copy_for_each(value, axis)
    return combined_pairwise(kept(pieces, identity, value), combine)


def cut_along(value, dim, length):
    before, after = (value.shape[:dim], value.shape[dim + 1 :])
    return jnp.moveaxis(value.reshape(*before, length, -1, *after), dim, 0)


def sum_at_owner(value, axis, dim):
    tiles = cut_along(value, dim, lax.axis_size(axis))
    arrived = lax.all_to_all(tiles, axis, split_axis=0, concat_axis=0, tiled=True)
    return arrived.sum(axis=0)


def in_one_piece(arrays, axis, dim, along):
    widths = [math.prod(a.shape[along:]) for a in arrays]
    both = jnp.concatenate(
        [a.reshape(*a.shape[:along], w) for a, w in zip(arrays, widths)], axis=along
    )
    whole = sum_at_owner(both, axis, dim)
    tiles = jnp.split(whole, [sum(widths[:k]) for k in range(1, len(widths))], axis=along)
    return tuple((b.reshape(*whole.shape[:along], *a.shape[along:]) for a, b in zip(arrays, tiles)))


def in_one_piece_2(arrays, axis, split_dim, concat_dim, along):
    columns = [a.reshape(*a.shape[:along], -1) for a in arrays]
    both = jnp.concatenate(columns, axis=along)
    whole, at, finished = (
        lax.all_to_all(both, axis, split_axis=split_dim, concat_axis=concat_dim, tiled=True),
        0,
        [],
    )
    for a, column in zip(arrays, columns):
        share = whole[..., at : at + column.shape[along]]
        finished.append(share.reshape(*share.shape[:along], *a.shape[along:]))
        at += column.shape[along]
    return tuple(finished)


def taken_together(value, axis):
    everything = copy_for_each(value, axis)
    return jnp.sum(everything, axis=0)


def side_by_side(arrays, axis, dim, along):
    widths = [math.prod(a.shape[along:]) for a in arrays]
    both = jnp.concatenate(
        [a.reshape(*a.shape[:along], w) for a, w in zip(arrays, widths)], axis=along
    )
    whole = lax.all_gather(both, axis, axis=dim, tiled=True)
    tiles = jnp.split(whole, [sum(widths[:k]) for k in range(1, len(widths))], axis=along)
    return tuple((b.reshape(*whole.shape[:along], *a.shape[along:]) for a, b in zip(arrays, tiles)))


def respond(queries, key_rows, values, gate_in, gate_forget, state_init, norm_init):
    key_scale = queries.shape[-1] ** (-0.5)
    length = queries.shape[0]
    cumulative = jnp.cumsum(jax.nn.log_sigmoid(gate_forget))
    scores = jnp.dot(queries, key_rows.T, preferred_element_type=jnp.float32) * key_scale
    target_positions = jnp.arange(length)
    causal = target_positions[:, None] >= target_positions[None, :]
    decays = jnp.where(causal, cumulative[:, None] - cumulative[None, :] + gate_in[None, :], -1e30)
    mixing = (scores * jnp.exp(decays)).astype(jnp.bfloat16)
    lifted = jnp.exp(cumulative) * key_scale
    numerator = jnp.dot(mixing, values, preferred_element_type=jnp.float32) + lifted[
        :, None
    ] * jnp.dot(queries, state_init, preferred_element_type=jnp.float32)
    denominator = jnp.dot(
        mixing, jnp.ones((length,), jnp.bfloat16), preferred_element_type=jnp.float32
    ) + lifted * jnp.dot(queries, norm_init, preferred_element_type=jnp.float32)
    return (numerator, denominator, lifted)


def add_terms(earlier, later_part):
    return earlier + later_part


def pick_sum(picked, source, extra):
    shaped = picked.reshape((1,) + picked.shape + (1,) * extra)
    return jnp.sum(jnp.where(shaped, source[:, None], 0.0), axis=2)


def local(
    prompt_keys,
    prompt_values,
    prompt_input,
    prompt_forget,
    prompt_lengths,
    response_prompt,
    resp_queries,
    resp_keys,
    resp_values,
    resp_input,
    resp_forget,
    norm_gain,
    out_grad,
):
    seq_index = lax.axis_index("seq")
    heads_here = prompt_input.shape[0]
    window_rows = prompt_keys.shape[0]
    key_width = prompt_keys.shape[1] // heads_here
    value_width = prompt_values.shape[1] // heads_here
    prompt_count = prompt_lengths.shape[0]
    resp_here = resp_queries.shape[0]
    resp_len = resp_queries.shape[1]
    positions = seq_index * window_rows + jnp.arange(window_rows, dtype=jnp.int32)
    prompt_ends = jnp.cumsum(prompt_lengths)
    prompt_id = jnp.sum((positions[:, None] >= prompt_ends[None, :]).astype(jnp.int32), axis=1)
    prompt_range = jnp.arange(prompt_count, dtype=jnp.int32)
    member = prompt_id[:, None] == prompt_range[None, :]
    member_f = member.astype(jnp.float32)
    log_forget = jax.nn.log_sigmoid(prompt_forget)
    masked = log_forget[:, :, None] * member_f[None]
    suffix = jnp.flip(jnp.cumsum(jnp.flip(masked, 1), 1), 1) - masked
    block_sums = jnp.sum(masked, axis=1)
    after_sums = carried_in(block_sums, "seq", add_terms, jnp.zeros_like(block_sums))
    weight = jnp.exp(
        prompt_input + jnp.sum((suffix + after_sums[:, None, :]) * member_f[None], axis=2)
    )
    key_rows3 = prompt_keys.reshape(window_rows, heads_here, key_width)
    value_rows3 = prompt_values.reshape(window_rows, heads_here, value_width)
    weighted = (key_rows3 * weight.T[:, :, None]).astype(jnp.bfloat16)
    block_rows = min(256, window_rows)
    block_count = window_rows // block_rows
    weighted_blocks = weighted.reshape(block_count, block_rows, heads_here, key_width)
    value_blocks = value_rows3.reshape(block_count, block_rows, heads_here, value_width)
    id_blocks = prompt_id.reshape(block_count, block_rows)
    member_blocks = member.reshape(block_count, block_rows, prompt_count)

    def state_step(carry, items):
        weight_row_block, value_row_block, rows_id, rows_member = items

        def state_single(unused):
            part = jnp.einsum(
                "xbp,xbi->bpi",
                weight_row_block,
                value_row_block,
                preferred_element_type=jnp.float32,
            )
            return jnp.where((prompt_range == rows_id[0])[None, :, None, None], part[:, None], 0.0)

        def state_several(unused):
            spread = jnp.where(
                rows_member[:, None, :, None],
                weight_row_block[:, :, None, :],
                jnp.zeros((), jnp.bfloat16),
            )
            return jnp.einsum(
                "thpk,thv->hpkv", spread, value_row_block, preferred_element_type=jnp.float32
            )

        added = lax.cond(rows_id[0] == rows_id[-1], state_single, state_several, 0)
        return (carry + added, None)

    states_init = jnp.zeros((heads_here, prompt_count, key_width, value_width), jnp.float32)
    states, unused_out = lax.scan(
        state_step, states_init, (weighted_blocks, value_blocks, id_blocks, member_blocks)
    )
    norms = jnp.einsum(
        "tp,thk->hpk", member.astype(jnp.bfloat16), weighted, preferred_element_type=jnp.float32
    )
    all_pick = response_prompt[:, 0][:, None] == prompt_range[None, :]
    share_states, share_norms = in_one_piece((states, norms), "seq", 2, 3)
    send_states = pick_sum(all_pick, share_states, 2).astype(jnp.bfloat16)
    send_norms = pick_sum(all_pick, share_norms, 1).astype(jnp.bfloat16)
    init_state, init_norm = in_one_piece_2((send_states, send_norms), "seq", 1, 2, 3)
    queries4 = resp_queries.reshape(resp_here, resp_len, heads_here, key_width)
    rkeys4 = resp_keys.reshape(resp_here, resp_len, heads_here, key_width)
    rvalues4 = resp_values.reshape(resp_here, resp_len, heads_here, value_width)
    per_response = jax.vmap(respond, in_axes=(0, 0, 0, 0, 0, 0, 0))
    per_head = jax.vmap(per_response, in_axes=(2, 2, 2, 0, 0, 0, 0))
    numerator, denominator, lifted = per_head(
        queries4, rkeys4, rvalues4, resp_input, resp_forget, init_state, init_norm
    )
    bound = jnp.sqrt(denominator * denominator + 1.0)
    hidden = numerator / bound[..., None]
    features = heads_here * value_width * lax.axis_size("head")
    total_squares = taken_together(jnp.sum(hidden * hidden, axis=(0, 3)), "head")
    inv_rms = lax.rsqrt(total_squares / features + 1e-06)
    gain = norm_gain.reshape(heads_here, value_width)[:, None, None, :]
    scaled = hidden * gain * inv_rms[None, :, :, None]
    resp_out = (
        jnp.transpose(scaled, (1, 2, 0, 3))
        .reshape(resp_here, resp_len, heads_here * value_width)
        .astype(jnp.bfloat16)
    )
    grad_heads = jnp.transpose(
        out_grad.reshape(resp_here, resp_len, heads_here, value_width), (2, 0, 1, 3)
    ).astype(jnp.float32)
    dots = taken_together(jnp.sum(grad_heads * gain * hidden, axis=(0, 3)), "head")
    d_hidden = (
        gain * grad_heads * inv_rms[None, :, :, None]
        - hidden * (dots * inv_rms**3 / features)[None, :, :, None]
    )
    d_numer = d_hidden / bound[..., None]
    d_denom = -jnp.sum(d_hidden * hidden, axis=-1) * denominator / (bound * bound)
    lift_numer = (lifted[..., None] * d_numer).astype(jnp.bfloat16)
    lift_denom = (lifted * d_denom).astype(jnp.bfloat16)
    d_state = jnp.einsum(
        "rlhk,hrlv->hrkv", queries4, lift_numer, preferred_element_type=jnp.float32
    )
    d_norm = jnp.einsum("rlhk,hrl->hrk", queries4, lift_denom, preferred_element_type=jnp.float32)
    all_by_prompt = all_pick.T
    slab_grad, slab_gnorm = tuple(
        (
            part.astype(jnp.float32)
            for part in in_one_piece_2(
                (d_state.astype(jnp.bfloat16), d_norm.astype(jnp.bfloat16)), "seq", 2, 1, 3
            )
        )
    )
    prompt_grad = jnp.sum(
        jnp.where(all_by_prompt[None, :, :, None, None], slab_grad[:, None], 0.0), axis=2
    )
    prompt_gnorm = jnp.sum(
        jnp.where(all_by_prompt[None, :, :, None], slab_gnorm[:, None], 0.0), axis=2
    )
    grad_low, gnorm_low = side_by_side(
        (prompt_grad.astype(jnp.bfloat16), prompt_gnorm.astype(jnp.bfloat16)), "seq", 2, 3
    )

    def grad_step(carry, items):
        weight_row_block, value_row_block, rows_id, rows_member = items

        def grad_single(unused):
            selected_rows = lax.dynamic_index_in_dim(grad_low, rows_id[0], 1, keepdims=False)
            selected_norm = lax.dynamic_index_in_dim(gnorm_low, rows_id[0], 1, keepdims=False)
            value_block_slice = jnp.einsum(
                "lrm,rmu->lru", weight_row_block, selected_rows, preferred_element_type=jnp.float32
            )
            key_block_slice = (
                jnp.einsum(
                    "ymz,mdz->ymd",
                    value_row_block,
                    selected_rows,
                    preferred_element_type=jnp.float32,
                )
                + selected_norm.astype(jnp.float32)[None]
            )
            return (key_block_slice, value_block_slice)

        def grad_several(unused):
            spread = jnp.where(
                rows_member[:, None, :, None],
                weight_row_block[:, :, None, :],
                jnp.zeros((), jnp.bfloat16),
            )
            value_block_slice = jnp.einsum(
                "thpk,hpkv->thv", spread, grad_low, preferred_element_type=jnp.float32
            )
            through = (
                jnp.einsum(
                    "thv,hpkv->thpk", value_row_block, grad_low, preferred_element_type=jnp.float32
                )
                + gnorm_low.astype(jnp.float32)[None]
            )
            key_block_slice = jnp.sum(
                jnp.where(rows_member[:, None, :, None], through, 0.0), axis=2
            )
            return (key_block_slice, value_block_slice)

        return (carry, lax.cond(rows_id[0] == rows_id[-1], grad_single, grad_several, 0))

    unused_carry, grads_out = lax.scan(
        grad_step, 0, (weighted_blocks, value_blocks, id_blocks, member_blocks)
    )
    key_blocks, value_grad_blocks = grads_out
    key_grad = key_blocks.reshape(window_rows, heads_here, key_width) * weight.T[:, :, None]
    value_grad = value_grad_blocks.reshape(window_rows, heads_here, value_width)
    prompt_key_grad = key_grad.reshape(window_rows, heads_here * key_width).astype(jnp.bfloat16)
    prompt_value_grad = value_grad.reshape(window_rows, heads_here * value_width).astype(
        jnp.bfloat16
    )
    return (resp_out, prompt_key_grad, prompt_value_grad)


def solution(mesh):
    in_specs = (
        P("seq", "head"),
        P("seq", "head"),
        P("head", "seq"),
        P("head", "seq"),
        P(),
        P(),
        P("seq", None, "head"),
        P("seq", None, "head"),
        P("seq", None, "head"),
        P("head", "seq", None),
        P("head", "seq", None),
        P("head"),
        P("seq", None, "head"),
    )
    out_specs = (P("seq", None, "head"), P("seq", "head"), P("seq", "head"))
    return jax.shard_map(local, mesh=mesh, in_specs=in_specs, out_specs=out_specs, check_vma=False)
```

profile of v0, /device:TPU:0, one launch (start us, length us, event | category | flops | bytes accessed | tf_op | source)
XLA Modules:
  0.0 279.8 jit_solution(1425157020388200133)
XLA Ops:
  9.6 8.0 %all-to-all-start = ((f32[16,1,4]{2,1,0:T(1,128)}), f32[16,1,4]{2,1,0:T(1,128)S(1)}, u32[]{:S(2)}, u32[]{:S(2)}) async-start(f32[16,1,4]{2,1,0:T(1,128)} %broadcast_in_dim.266), calls=%async_computation | async-start | bytes 16384 | tf_op jit(solution)/shard_map/all_to_all | solution.py:11
  21.3 3.9 %all-to-all-done = f32[16,1,4]{2,1,0:T(1,128)S(1)} async-done(((f32[16,1,4]{2,1,0:T(1,128)}), f32[16,1,4]{2,1,0:T(1,128)S(1)}, u32[]{:S(2)}, u32[]{:S(2)}) %all-to-all-start) | async-done | bytes 288 | tf_op jit(solution)/shard_map/all_to_all | solution.py:11
  26.1 2.0 multiply_convert_fusion.3
  28.2 2.1 convolution_bitcast_fusion.5
  30.2 48.7 %while.28 = (s32[]{:T(128)}, f32[1,4,256,512]{3,2,1,0:T(8,128)}, s32[4,256]{1,0:T(4,128)}, bf16[4,256,1,256]{3,1,2,0:T(8,128)(2,1)}, bf16[4,256,1,512]{3,1,2,0:T(8,128)(2,1)}, /*index=5*/s32[]{:T(128)}, s32[]{:T(128)}, s32[]{}) while((s32[]{:T(128)}, f32[1,4,256,512]{3,2,1,0:T(8,128)}, ...), condition=%wide.region_11.12_spmd.clone.clone.clone, body=%wide.region_8.11_spmd.clone.clone.clone.sunk | while | flops 269747200 | bytes 10635553 | solution.py:188
  32.1 1.3 constant_dynamic-slice_fusion.9
  33.9 1.3 fusion.78
  36.5 3.0 %conditional.10 = (f32[1,4,256,512]{3,2,1,0:T(8,128)S(1)}) conditional(s32[]{:T(128)} %bitcast.250, (s32[4,256]{1,0:T(4,128)}, s32[]{:T(128)}, bf16[256,1,256]{2,0,1:T(8,128)(2,1)S(1)}, bf16[256,1,512]{2,0,1:T(8,128)(2,1)S(1)}, s32[4,256,4]{1,2,0:T(4,128)S(1)}) %tuple.138, (s32[1,256]{1,0:T(1,128)}, s32[4]{0:T(128)}, ...), branch_computations={%region_9.9_spmd, %region_10.10_spmd} | conditional | flops 268698624 | bytes 3538988 | solution.py:184
  39.5 1.9 select_add_fusion.2
  45.1 1.3 fusion.78
  47.6 2.5 conditional.10
  50.1 3.4 %select_add_fusion.2 = f32[1,4,256,512]{3,2,1,0:T(8,128)} fusion(f32[1,4,256,512]{3,2,1,0:T(8,128)S(1)} %get-tuple-element.647, f32[1,4,256,512]{3,2,1,0:T(8,128)} %get-tuple-element.599, pred[]{:T(512)S(6)} %compare.5), kind=kLoop, calls=%fused_computation.55.clone.1 | loop fusion | flops 1048576 | bytes 6291457 | tf_op jit(solution)/shard_map/while/body/eval_jaxpr/add | solution.py:185
  57.3 1.3 fusion.78
  59.8 3.0 %conditional.10 = (f32[1,4,256,512]{3,2,1,0:T(8,128)S(1)}) conditional(s32[]{:T(128)} %bitcast.250, (s32[4,256]{1,0:T(4,128)}, s32[]{:T(128)}, bf16[256,1,256]{2,0,1:T(8,128)(2,1)S(1)}, bf16[256,1,512]{2,0,1:T(8,128)(2,1)S(1)}, s32[4,256,4]{1,2,0:T(4,128)S(1)}) %tuple.138, (s32[1,256]{1,0:T(1,128)}, s32[4]{0:T(128)}, ...), branch_computations={%region_9.9_spmd, %region_10.10_spmd} | conditional | flops 268698624 | bytes 3538988 | solution.py:184
  62.8 3.4 %select_add_fusion.2 = f32[1,4,256,512]{3,2,1,0:T(8,128)} fusion(f32[1,4,256,512]{3,2,1,0:T(8,128)S(1)} %get-tuple-element.647, f32[1,4,256,512]{3,2,1,0:T(8,128)} %get-tuple-element.599, pred[]{:T(512)S(6)} %compare.5), kind=kLoop, calls=%fused_computation.55.clone.1 | loop fusion | flops 1048576 | bytes 6291457 | tf_op jit(solution)/shard_map/while/body/eval_jaxpr/add | solution.py:185
  70.0 1.3 fusion.78
  72.5 3.0 %conditional.10 = (f32[1,4,256,512]{3,2,1,0:T(8,128)S(1)}) conditional(s32[]{:T(128)} %bitcast.250, (s32[4,256]{1,0:T(4,128)}, s32[]{:T(128)}, bf16[256,1,256]{2,0,1:T(8,128)(2,1)S(1)}, bf16[256,1,512]{2,0,1:T(8,128)(2,1)S(1)}, s32[4,256,4]{1,2,0:T(4,128)S(1)}) %tuple.138, (s32[1,256]{1,0:T(1,128)}, s32[4]{0:T(128)}, ...), branch_computations={%region_9.9_spmd, %region_10.10_spmd} | conditional | flops 268698624 | bytes 3538988 | solution.py:184
  75.5 3.4 %select_add_fusion.2 = f32[1,4,256,512]{3,2,1,0:T(8,128)} fusion(f32[1,4,256,512]{3,2,1,0:T(8,128)S(1)} %get-tuple-element.647, f32[1,4,256,512]{3,2,1,0:T(8,128)} %get-tuple-element.599, pred[]{:T(512)S(6)} %compare.5), kind=kLoop, calls=%fused_computation.55.clone.1 | loop fusion | flops 1048576 | bytes 6291457 | tf_op jit(solution)/shard_map/while/body/eval_jaxpr/add | solution.py:185
  80.0 1.9 maximum_bitcast_fusion
  81.9 1.8 copy.161
  83.7 4.6 %all-to-all-start.1 = ((f32[16,1,4,16,513]{4,3,2,1,0:T(8,128)}), f32[16,1,4,16,513]{4,3,2,1,0:T(8,128)}, u32[]{:S(2)}, u32[]{:S(2)}) async-start(f32[16,1,4,16,513]{4,3,2,1,0:T(8,128)} %copy.161), calls=%async_computation.1 | async-start | bytes 5242880 | tf_op jit(solution)/shard_map/all_to_all | solution.py:43
  90.2 2.0 multiply_convert_fusion.2
  92.2 31.1 %all-to-all-done.1 = f32[16,1,4,16,513]{4,3,2,1,0:T(8,128)} async-done(((f32[16,1,4,16,513]{4,3,2,1,0:T(8,128)}), f32[16,1,4,16,513]{4,3,2,1,0:T(8,128)}, u32[]{:S(2)}, u32[]{:S(2)}) %all-to-all-start.1) | async-done | bytes 2101280 | tf_op jit(solution)/shard_map/all_to_all | solution.py:43
  123.3 1.9 reduce_sum.134
  127.0 4.3 %all-to-all-start.2 = ((bf16[1,32,16,513]{3,2,0,1:T(8,128)(2,1)}), bf16[1,32,16,513]{3,2,0,1:T(8,128)(2,1)}, u32[]{:S(2)}, u32[]{:S(2)}) async-start(bf16[1,32,16,513]{3,2,0,1:T(8,128)(2,1)} %maximum_bitcast_fusion.1), calls=%async_computation.2 | async-start | bytes 1310720 | tf_op jit(solution)/shard_map/all_to_all | solution.py:61
  131.7 2.1 fusion.63
  133.8 8.3 %all-to-all-done.2 = bf16[1,32,16,513]{3,2,0,1:T(8,128)(2,1)} async-done(((bf16[1,32,16,513]{3,2,0,1:T(8,128)(2,1)}), bf16[1,32,16,513]{3,2,0,1:T(8,128)(2,1)}, u32[]{:S(2)}, u32[]{:S(2)}) %all-to-all-start.2) | async-done | bytes 525344 | tf_op jit(solution)/shard_map/all_to_all | solution.py:61
  143.4 1.3 fusion.64
  144.7 4.1 %multiply_reduce_fusion.1 = (f32[2,512]{1,0:T(2,128)S(1)}, f32[2,512]{1,0:T(2,128)S(1)}, f32[2,512,512]{1,2,0:T(8,128)}) fusion(bf16[2,512,512]{1,2,0:T(8,128)(2,1)S(1)} %copy.168, f32[512]{0:T(512)S(1)} %copy-done.8, f32[2,512]{1,0:T(2,128)S(1)} %add_sqrt_fusion, f32[2,512,512]{1,2,0:T(8,128)} %fusion.63, bf16[2,512,256]{2,1,0:T(8,128)(2,1)} %param.27, ...), kind=kOutput, calls=%fused_computation.68 | convolution fusion | flops 273152000 | bytes 6309888 | tf_op jit(solution)/shard_map/vmap(vmap())/dot_general | solution.py:99
  148.9 9.7 %all_to_all.56 = f32[8,2,512]{2,1,0:T(2,128)S(1)} all-to-all(f32[8,2,512]{2,1,0:T(2,128)S(1)} %broadcast_in_dim.276), channel_id=1, replica_groups=mesh['seq'=16,'head'=8] {'head'}, dimensions={0} | all-to-all | bytes 65536 | tf_op jit(solution)/shard_map/all_to_all | solution.py:11
  159.2 3.3 %all-to-all-start.4 = ((f32[8,2,512]{2,1,0:T(2,128)}), f32[8,2,512]{2,1,0:T(2,128)S(1)}, u32[]{:S(2)}, u32[]{:S(2)}) async-start(f32[8,2,512]{2,1,0:T(2,128)} %broadcast_in_dim.280), calls=%async_computation.4 | async-start | bytes 65536 | tf_op jit(solution)/shard_map/all_to_all | solution.py:11
  162.6 5.3 %all-to-all-done.4 = f32[8,2,512]{2,1,0:T(2,128)S(1)} async-done(((f32[8,2,512]{2,1,0:T(2,128)}), f32[8,2,512]{2,1,0:T(2,128)S(1)}, u32[]{:S(2)}, u32[]{:S(2)}) %all-to-all-start.4) | async-done | bytes 32800 | tf_op jit(solution)/shard_map/all_to_all | solution.py:11
  168.0 2.4 fusion.40
  171.7 1.8 copy.171
  173.5 3.6 %all-to-all-start.5 = ((bf16[1,2,256,513]{3,1,0,2:T(2,128)(2,1)}), bf16[1,2,256,513]{3,1,0,2:T(2,128)(2,1)S(1)}, u32[]{:S(2)}, u32[]{:S(2)}) async-start(bf16[1,2,256,513]{3,1,0,2:T(2,128)(2,1)} %copy.171), calls=%async_computation.5 | async-start | bytes 1310720 | tf_op jit(solution)/shard_map/all_to_all | solution.py:61
  177.4 12.8 %all-to-all-done.5 = bf16[1,2,256,513]{3,1,0,2:T(2,128)(2,1)S(1)} async-done(((bf16[1,2,256,513]{3,1,0,2:T(2,128)(2,1)}), bf16[1,2,256,513]{3,1,0,2:T(2,128)(2,1)S(1)}, u32[]{:S(2)}, u32[]{:S(2)}) %all-to-all-start.5) | async-done | bytes 525344 | tf_op jit(solution)/shard_map/all_to_all | solution.py:61
  192.0 1.3 copy.181
  193.3 38.1 %all-gather.2.cloned.1.call-done = bf16[1,4,256,513]{3,1,0,2:T(4,128)(2,1)} async-done(((bf16[1,4,16,513]{3,1,0,2:T(4,128)(2,1)}), bf16[1,4,256,513]{3,1,0,2:T(4,128)(2,1)}) %all-gather.2.cloned.1.call-update) | async-done | bytes 1050640 | tf_op jit(solution)/shard_map/all_gather | solution.py:82
  233.0 37.7 %while.27 = (s32[]{:T(128)}, f32[4,256,1,256]{3,1,0,2:T(8,128)}, bf16[4,256,1,512]{3,1,2,0:T(8,128)(2,1)}, s32[4,256]{1,0:T(4,128)}, bf16[4,256,1,256]{3,1,2,0:T...) while((s32[]{:T(128)}, f32[4,256,1,256]{3,1,0,2:T(8,128)}, ...), condition=%wide.region_26.27_spmd.clone.clone, body=%wide.region_22.26_spmd.clone.clone.sunk | while | flops 537856000 | bytes 5414179 | solution.py:296
  235.6 1.3 fusion.77
  238.1 3.1 %conditional.9 = (f32[1,256,1,256]{1,3,2,0:T(8,128)S(1)}, bf16[1,256,1,512]{3,1,2,0:T(8,128)(2,1)S(1)}) conditional(s32[]{:T(128)} %bitcast.247, (s32[4,256]{1,0:T(4,128)}, s32[]{:T(128)}, bf16[1,4,256,512]{3,2,1,0:T(8,128)(2,1)S(1)}, bf16[256,1,512]{2,0,1:T(8,128)(2,1)S(1)}, bf16[1,4,256]{2,1,0:T(4,128)(2,1)S(1)}, ...), branch_computations={%region_23.24_spmd, %region_25.25_spmd} | conditional | flops 537856000 | bytes 3035160 | solution.py:294
  245.4 1.3 fusion.77
  247.9 1.7 conditional.9
  253.8 1.3 fusion.77
  256.2 3.1 %conditional.9 = (f32[1,256,1,256]{1,3,2,0:T(8,128)S(1)}, bf16[1,256,1,512]{3,1,2,0:T(8,128)(2,1)S(1)}) conditional(s32[]{:T(128)} %bitcast.247, (s32[4,256]{1,0:T(4,128)}, s32[]{:T(128)}, bf16[1,4,256,512]{3,2,1,0:T(8,128)(2,1)S(1)}, bf16[256,1,512]{2,0,1:T(8,128)(2,1)S(1)}, bf16[1,4,256]{2,1,0:T(4,128)(2,1)S(1)}, ...), branch_computations={%region_23.24_spmd, %region_25.25_spmd} | conditional | flops 537856000 | bytes 3035160 | solution.py:294
  263.5 1.3 fusion.77
  266.0 3.1 %conditional.9 = (f32[1,256,1,256]{1,3,2,0:T(8,128)S(1)}, bf16[1,256,1,512]{3,1,2,0:T(8,128)(2,1)S(1)}) conditional(s32[]{:T(128)} %bitcast.247, (s32[4,256]{1,0:T(4,128)}, s32[]{:T(128)}, bf16[1,4,256,512]{3,2,1,0:T(8,128)(2,1)S(1)}, bf16[256,1,512]{2,0,1:T(8,128)(2,1)S(1)}, bf16[1,4,256]{2,1,0:T(4,128)(2,1)S(1)}, ...), branch_computations={%region_23.24_spmd, %region_25.25_spmd} | conditional | flops 537856000 | bytes 3035160 | solution.py:294
  270.7 2.2 fusion.41
  (190 shorter events, 65.9 us)
Async XLA Ops:
  7.2 124.5 %copy-start = (bf16[2,512,512]{2,1,0:T(8,128)(2,1)S(1)}, bf16[2,512,512]{2,1,0:T(8,128)(2,1)}, u32[]{:S(2)}) copy-start(bf16[2,512,512]{2,1,0:T(8,128)(2,1)} %param.29) | copy-start | bytes 3145732
  9.6 15.5 %all-to-all-start = ((f32[16,1,4]{2,1,0:T(1,128)}), f32[16,1,4]{2,1,0:T(1,128)S(1)}, u32[]{:S(2)}, u32[]{:S(2)}) async-start(f32[16,1,4]{2,1,0:T(1,128)} %broadcast_in_dim.266), calls=%async_computation | async-start | bytes 16384 | tf_op jit(solution)/shard_map/all_to_all | solution.py:11
  26.1 4.1 %copy-start.5 = (f32[1,1024]{1,0:T(1,128)}, f32[1,1024]{1,0:T(1,128)S(1)}, u32[]{:S(2)}) copy-start(f32[1,1024]{1,0:T(1,128)S(1)} %add_exponential_fusion) | copy-start | bytes 12292
  83.7 4.6 %copy-start.10 = (s32[32,1]{0,1:T(1,128)S(1)}, s32[32,1]{0,1:T(1,128)}, u32[]{:S(2)}) copy-start(s32[32,1]{0,1:T(1,128)} %param.26) | copy-start | bytes 388
  83.7 4.7 %copy-start.7 = (f32[1,2,512]{2,1,0:T(2,128)S(1)}, f32[1,2,512]{2,1,0:T(2,128)}, u32[]{:S(2)}) copy-start(f32[1,2,512]{2,1,0:T(2,128)} %param.31) | copy-start | bytes 12292
  83.7 5.7 %copy-start.4 = (bf16[2,512,512]{2,1,0:T(8,128)(2,1)S(1)}, bf16[2,512,512]{2,1,0:T(8,128)(2,1)}, u32[]{:S(2)}) copy-start(bf16[2,512,512]{2,1,0:T(8,128)(2,1)} %param.33) | copy-start | bytes 3145732
  83.7 39.6 %all-to-all-start.1 = ((f32[16,1,4,16,513]{4,3,2,1,0:T(8,128)}), f32[16,1,4,16,513]{4,3,2,1,0:T(8,128)}, u32[]{:S(2)}, u32[]{:S(2)}) async-start(f32[16,1,4,16,513]{4,3,2,1,0:T(8,128)} %copy.161), calls=%async_computation.1 | async-start | bytes 5242880 | tf_op jit(solution)/shard_map/all_to_all | solution.py:43
  88.3 1.9 copy-start.9
  127.0 15.1 %all-to-all-start.2 = ((bf16[1,32,16,513]{3,2,0,1:T(8,128)(2,1)}), bf16[1,32,16,513]{3,2,0,1:T(8,128)(2,1)}, u32[]{:S(2)}, u32[]{:S(2)}) async-start(bf16[1,32,16,513]{3,2,0,1:T(8,128)(2,1)} %maximum_bitcast_fusion.1), calls=%async_computation.2 | async-start | bytes 1310720 | tf_op jit(solution)/shard_map/all_to_all | solution.py:61
  131.7 13.0 %copy-start.8 = (f32[512]{0:T(512)S(1)}, f32[512]{0:T(512)}, u32[]{:S(2)}) copy-start(f32[512]{0:T(512)} %param.32) | copy-start | bytes 6148
  144.7 23.3 %copy-start.2 = (bf16[2,512,256]{2,1,0:T(8,128)(2,1)S(1)}, bf16[2,512,256]{2,1,0:T(8,128)(2,1)}, u32[]{:S(2)}) copy-start(bf16[2,512,256]{2,1,0:T(8,128)(2,1)} %param.27) | copy-start | bytes 1572868
  159.2 8.7 %all-to-all-start.4 = ((f32[8,2,512]{2,1,0:T(2,128)}), f32[8,2,512]{2,1,0:T(2,128)S(1)}, u32[]{:S(2)}, u32[]{:S(2)}) async-start(f32[8,2,512]{2,1,0:T(2,128)} %broadcast_in_dim.280), calls=%async_computation.4 | async-start | bytes 65536 | tf_op jit(solution)/shard_map/all_to_all | solution.py:11
  168.0 2.5 copy-start.1
  170.5 1.0 copy-start.3
  173.5 16.7 %all-to-all-start.5 = ((bf16[1,2,256,513]{3,1,0,2:T(2,128)(2,1)}), bf16[1,2,256,513]{3,1,0,2:T(2,128)(2,1)S(1)}, u32[]{:S(2)}, u32[]{:S(2)}) async-start(bf16[1,2,256,513]{3,1,0,2:T(2,128)(2,1)} %copy.171), calls=%async_computation.5 | async-start | bytes 1310720 | tf_op jit(solution)/shard_map/all_to_all | solution.py:61
  177.1 54.3 %all-gather.2.cloned.1.call-start = ((), (), s32[]{:S(2)}) async-start(), calls=%async_computation.6 | async-start | bytes 1392640 | tf_op jit(solution)/shard_map/all_gather | solution.py:82
  231.4 1.2 slice-start
  231.4 1.4 slice-start.1
  233.0 37.7 %copy-start.6 = (f32[1,1024]{1,0:T(1,128)S(1)}, f32[1,1024]{1,0:T(1,128)}, u32[]{:S(2)}) copy-start(f32[1,1024]{1,0:T(1,128)} %copy-done.5) | copy-start | bytes 12292
Sparse Core Ops, SparseCore 0:
  192.1 39.2 all-gather.1
where the time goes:
time: 283 us; the launch traced here: 280 us
  waiting for transfers between devices  99.6 us (35%)
  local copies, waits for them, and re-layouts  63.6 us (22%)
  other arithmetic  33.6 us (12%)
  starting transfers between devices  24 us (8%)
  matrix products  19 us (7%)
  loops' own time  15.8 us (6%)
  between operations  14.5 us (5%)
  blocking collectives  9.71 us (3%)
    all_gather x1, waiting for transfers between devices, side_by_side(): whole = lax.all_gather(both, axis, axis=dim, tiled=True)  38.1 us
    all_to_all x1, waiting for transfers between devices, sum_at_owner(): lax.all_to_all(tiles, axis, split_axis=0, concat_axis=0, tiled=True)  31.1 us
    all_to_all x2, waiting for transfers between devices, in_one_piece_2(): lax.all_to_all(both, axis, split_axis=split_dim, concat_axis=concat_dim,...  21.1 us
    squeeze x16, local copies, waits for them, and re-layouts, local(): lax.scan(state_step, states_init, (weighted_blocks, value_blocks, id_bloc...  15.1 us
    add x4, other arithmetic, state_step(): return (carry + added, None)  12.2 us
    all_to_all x2, starting transfers between devices, copy_for_each(): lax.all_to_all(jnp.broadcast_to(value[None], (length, *value.shape)), axi...  11.3 us
    all_to_all x1, blocking collectives, copy_for_each(): lax.all_to_all(jnp.broadcast_to(value[None], (length, *value.shape)), axi...  9.71 us
    all_to_all x2, waiting for transfers between devices, copy_for_each(): lax.all_to_all(jnp.broadcast_to(value[None], (length, *value.shape)), axi...  9.21 us
  transfers between devices with their start and end apart: 6, of which 6 were waited for; matrix products, arithmetic and copies ran while one was open for 4% of the time, Pallas kernels for 0%

commit v1 on v0

v1 whole, which is shorter than its diff:
```python
import functools

import jax
import jax.numpy as jnp
from jax import lax
from jax.experimental import pallas as pl
from jax.experimental.pallas import tpu as pltpu
from jax.sharding import PartitionSpec as P

F32 = jnp.float32
BF16 = jnp.bfloat16
PROMPTS = 4
SEQ = 16
HEADS = 8
DK = 256
DV = 512
WIN = 1024
RLEN = 512
ROWS = DK // SEQ
AUX = 8
LANES = 128
SCALE = DK ** (-0.5)

VMEM = pl.BlockSpec(memory_space=pltpu.VMEM)
SMEM = pl.BlockSpec(memory_space=pltpu.SMEM)


def call(body, ins, outs, scratch, **kw):
    return pl.pallas_call(
        body,
        in_specs=ins,
        out_specs=tuple(VMEM for _ in outs),
        out_shape=tuple(jax.ShapeDtypeStruct(s, d) for s, d in outs),
        scratch_shapes=scratch,
        compiler_params=pltpu.CompilerParams(vmem_limit_bytes=48 << 20),
        **kw,
    )


def iota(shape, dim):
    return lax.broadcasted_iota(jnp.int32, shape, dim)


def ends_of(len_ref):
    e0 = len_ref[0]
    e1 = e0 + len_ref[1]
    e2 = e1 + len_ref[2]
    return e0, e1, e2


def prompt_at(position, ends):
    total = 0
    for e in ends:
        total = total + (position >= e).astype(jnp.int32)
    return total


def first_prompt(device, ends, slots):
    if slots == PROMPTS:
        return 0
    total = jnp.int32(0)
    for e in ends:
        total = total + jnp.where(device * WIN >= e, 1, 0)
    return total


def log_sigmoid(x):
    return jnp.minimum(x, 0.0) - jnp.log1p(jnp.exp(-jnp.abs(x)))


def dot(a, b, ca, cb):
    return lax.dot_general(a, b, (((ca,), (cb,)), ((), ())), preferred_element_type=F32)


def split_two(x):
    hi = x.astype(BF16)
    return hi, (x - hi.astype(F32)).astype(BF16)


def whole(x):
    return jnp.sum(jnp.sum(x, axis=0, keepdims=True), axis=1, keepdims=True)


def window_pid(me, ends):
    shape = (WIN // LANES, LANES)
    return prompt_at(me * WIN + iota(shape, 0) * LANES + iota(shape, 1), ends)


def state_kernel(slots, len_ref, pk, pv, pin, pf, msg, e_out, gates, inputs, wmat):
    me = lax.axis_index("seq")
    ends = ends_of(len_ref)
    groups = WIN // LANES
    for r in range(groups):
        gates[r : r + 1, :] = pf[:, r * LANES : (r + 1) * LANES]
        inputs[r : r + 1, :] = pin[:, r * LANES : (r + 1) * LANES]
    shape = (groups, LANES)
    pid = window_pid(me, ends)
    lane, row = iota(shape, 1), iota(shape, 0)
    lf = log_sigmoid(gates[...])
    tail = lf
    step = 1
    while step < LANES:
        tail = tail + jnp.where(lane < LANES - step, pltpu.roll(tail, LANES - step, 1), 0.0)
        step *= 2
    after = jnp.broadcast_to(tail[:, 0:1], shape)
    after = jnp.where(row < groups - 1, pltpu.roll(after, groups - 1, 0), 0.0)
    step = 1
    while step < groups:
        after = after + jnp.where(row < groups - step, pltpu.roll(after, groups - step, 0), 0.0)
        step *= 2
    sums = [whole(jnp.where(pid == p, lf, 0.0)) for p in range(PROMPTS)]
    later = jnp.where(
        pid == 0,
        sums[1] + sums[2] + sums[3],
        jnp.where(pid == 1, sums[2] + sums[3], jnp.where(pid == 2, sums[3], 0.0)),
    )
    expo = inputs[...] + ((tail - lf) + after - later)
    e_out[...] = expo
    weight = jnp.exp(expo)
    first = first_prompt(me, ends, slots)
    stacked = jnp.concatenate(
        [jnp.where(pid == first + s, weight, 0.0) for s in range(slots)], axis=0
    )
    if slots * groups < LANES:
        stacked = jnp.concatenate(
            [stacked, jnp.zeros((LANES - slots * groups, LANES), F32)], axis=0
        )
    columns = stacked.T
    for r in range(groups):
        rows = slice(r * LANES, (r + 1) * LANES)
        keys = pk[rows, :].astype(F32)
        for s in range(slots):
            at = s * groups + r
            wmat[s, rows, :] = (keys * columns[:, at : at + 1]).astype(BF16)
    for s in range(slots):
        state = dot(wmat[s], pv[...], 0, 0).astype(BF16)
        for dev in range(SEQ):
            msg[dev, s * ROWS : (s + 1) * ROWS, :] = state[dev * ROWS : (dev + 1) * ROWS, :]
    ashape = (AUX, DV)
    arow, alane = iota(ashape, 0), iota(ashape, 1)
    aux = jnp.zeros(ashape, F32)
    for p in range(PROMPTS):
        rest = jnp.broadcast_to(sums[p], ashape)
        for part in range(3):
            piece = rest.astype(BF16).astype(F32)
            aux = jnp.where((arow == 4 + part) & (alane == p), piece, aux)
            rest = rest - piece
    aux = aux.astype(BF16)
    for dev in range(SEQ):
        msg[dev, slots * ROWS : slots * ROWS + AUX, :] = aux


def spread_kernel(slots, len_ref, rp, m, expo, pk, out, aft, acc, low, afters):
    me = lax.axis_index("seq")
    ends = ends_of(len_ref)
    shape = (SEQ, LANES)
    lane, row = iota(shape, 1), iota(shape, 0)
    base = slots * ROWS
    gates = m[:, base : base + AUX, 0:LANES].astype(F32)
    sums = gates[:, 6, :] + gates[:, 5, :] + gates[:, 4, :]
    after = jnp.where(row < SEQ - 1, pltpu.roll(sums, SEQ - 1, 0), 0.0)
    step = 1
    while step < SEQ:
        after = after + jnp.where(row < SEQ - step, pltpu.roll(after, SEQ - step, 0), 0.0)
        step *= 2
    afters[...] = after
    mine = jnp.broadcast_to(afters[pl.ds(me, 1), :], aft.shape)
    aft[...] = mine
    factor = jnp.exp(after)
    if slots == PROMPTS:
        first = jnp.zeros(shape, jnp.int32)
    else:
        first = prompt_at(row * WIN, ends)
    acc[...] = jnp.zeros_like(acc)
    for s in range(slots):
        scale = jnp.sum(jnp.where(lane == first + s, factor, 0.0), axis=1, keepdims=True)
        for dev in range(SEQ):
            p = first_prompt(dev, ends, slots) + s
            f = scale[dev : dev + 1, :]
            acc[p] += f * m[dev, s * ROWS : (s + 1) * ROWS, :].astype(F32)
    for p in range(PROMPTS):
        low[p] = acc[p].astype(BF16)
    groups = WIN // LANES
    pid = window_pid(me, ends)
    rest = jnp.zeros((groups, LANES), F32)
    for p in range(PROMPTS):
        rest = jnp.where(pid == p, mine[0:1, p : p + 1], rest)
    weight = jnp.exp(expo[...] + rest)
    columns = jnp.concatenate([weight, jnp.zeros((LANES - groups, LANES), F32)], axis=0).T
    mrow = iota((8, LANES), 0)
    norms = jnp.zeros((8, DK), F32)
    for r in range(groups):
        weighted = pk[r * LANES : (r + 1) * LANES, :].astype(F32) * columns[:, r : r + 1]
        member = (jnp.broadcast_to(pid[r : r + 1, :], (8, LANES)) == mrow).astype(F32)
        norms = norms + dot(member.astype(BF16), weighted.astype(BF16), 1, 0)
    aux = jnp.zeros((AUX, DV), F32)
    arow = iota((AUX, DV), 0)
    for part, piece in enumerate(split_two(norms)):
        piece = piece.astype(F32)
        for pair in range(PROMPTS // 2):
            both = jnp.concatenate(
                [piece[2 * pair : 2 * pair + 1, :], piece[2 * pair + 1 : 2 * pair + 2, :]], axis=1
            )
            aux = jnp.where(arow == 2 * part + pair, both, aux)
    aux = aux.astype(BF16)
    for dev in range(SEQ):
        for r in range(2):
            out[dev, r * ROWS : (r + 1) * ROWS, :] = low[rp[2 * dev + r, 0]]
        out[dev, 2 * ROWS : 2 * ROWS + AUX, :] = aux


def respond_kernel(q, k, v, rin, rf, num, cols):
    shape = (8, RLEN)
    row, lane = iota(shape, 0), iota(shape, 1)
    gate = jnp.where(row == 0, rf[0, 0:1, :], rf[0, 1:2, :])
    cum = log_sigmoid(gate)
    step = 1
    while step < RLEN:
        cum = cum + jnp.where(lane >= step, pltpu.roll(cum, step, 1), 0.0)
        step *= 2
    tall = jnp.concatenate([cum, jnp.zeros((LANES - 8, RLEN), F32)], axis=0).T
    half = RLEN // 2
    clane = iota((RLEN, LANES), 1)
    packed = jnp.zeros((RLEN, LANES), F32)
    for r in range(2):
        ccol = tall[:, r : r + 1]
        srow = rin[0, r : r + 1, :] - cum[r : r + 1, :]
        for b in range(2):
            rows = slice(b * half, (b + 1) * half)
            width = (b + 1) * half
            scores = dot(q[r, rows, :], k[r, 0:width, :], 1, 1) * SCALE
            causal = iota((half, width), 0) + b * half >= iota((half, width), 1)
            decay = jnp.where(causal, ccol[rows, :] + srow[:, 0:width], -1e30)
            mixing = (scores * jnp.exp(decay)).astype(BF16)
            num[r, rows, :] = dot(mixing, v[r, 0:width, :], 1, 0)
            den = jnp.sum(mixing.astype(F32), axis=1, keepdims=True)
            cols[rows, :] = jnp.where(
                clane[rows, :] == r, den, packed[rows, :] if r == 0 else cols[rows, :]
            )
        lifted = jnp.exp(ccol) * SCALE
        cols[...] = jnp.where(clane == 2 + r, lifted, cols[...])


def hidden_kernel(rp, q, m, num, cols, og, gain, hid, cols2, msg, nrm):
    me = lax.axis_index("seq")
    aux = jnp.sum(m[:, 2 * ROWS : 2 * ROWS + AUX, :].astype(F32), axis=0)
    for p in range(PROMPTS):
        side = slice((p % 2) * DK, (p % 2 + 1) * DK)
        at = p // 2
        nrm[p : p + 1, :] = aux[at : at + 1, side] + aux[at + 2 : at + 3, side]
    clane = iota((RLEN, LANES), 1)
    sums = jnp.zeros((RLEN, LANES), F32)
    packed = jnp.zeros((RLEN, LANES), F32)
    for r in range(2):
        state = m[:, r * ROWS : (r + 1) * ROWS, :].reshape(DK, DV)
        norm = jnp.broadcast_to(nrm[pl.ds(rp[2 * me + r, 0], 1), :], (LANES, DK)).astype(BF16)
        lifted = cols[:, 2 + r : 3 + r]
        qn = dot(q[r], norm, 1, 1)[:, 0:1]
        den = cols[:, r : r + 1] + lifted * qn
        inverse = 1.0 / jnp.sqrt(den * den + 1.0)
        hidden = (num[r] + lifted * dot(q[r], state, 1, 0)) * inverse
        hid[r] = hidden
        squares = jnp.sum(hidden * hidden, axis=1, keepdims=True)
        dots = jnp.sum(og[r].astype(F32) * gain[...] * hidden, axis=1, keepdims=True)
        sums = jnp.where(clane == 2 * r, squares, jnp.where(clane == 2 * r + 1, dots, sums))
        lift = lifted * inverse
        ratio = lifted * den * (inverse * inverse)
        packed = jnp.where(clane == 4 + r, lift, jnp.where(clane == 6 + r, ratio, packed))
    cols2[...] = packed + sums
    rows = sums.T[0:8, :]
    for dev in range(HEADS):
        msg[dev] = rows


def grad_kernel(m, hid, cols2, og, gain, q, out, msg):
    total = m[0]
    for dev in range(1, HEADS):
        total = total + m[dev]
    features = HEADS * DV
    lists = []
    for r in range(2):
        inv = lax.rsqrt(total[2 * r : 2 * r + 1, :] / features + 1e-6)
        lists += [inv, total[2 * r + 1 : 2 * r + 2, :] * (inv * inv * inv) / features]
    rows = jnp.concatenate(lists + [jnp.zeros((LANES - 4, RLEN), F32)], axis=0)
    tall = rows.T
    norms = []
    for r in range(2):
        inv, coef = tall[:, 2 * r : 2 * r + 1], tall[:, 2 * r + 1 : 2 * r + 2]
        squares, dots = cols2[:, 2 * r : 2 * r + 1], cols2[:, 2 * r + 1 : 2 * r + 2]
        lift, ratio = cols2[:, 4 + r : 5 + r], cols2[:, 6 + r : 7 + r]
        hidden = hid[r]
        out[r] = (hidden * gain[...] * inv).astype(BF16)
        d_hidden = gain[...] * og[r].astype(F32) * inv - hidden * coef
        lift_numer = (lift * d_hidden).astype(BF16)
        lift_denom = (-(inv * dots - coef * squares) * ratio).astype(BF16).astype(F32)
        state = dot(q[r], lift_numer, 0, 0).astype(BF16)
        for dev in range(SEQ):
            msg[dev, r * ROWS : (r + 1) * ROWS, :] = state[dev * ROWS : (dev + 1) * ROWS, :]
        norms.append(split_two(jnp.sum(lift_denom * q[r].astype(F32), axis=0, keepdims=True)))
    arow = iota((AUX, DV), 0)
    aux = jnp.zeros((AUX, DV), F32)
    for part in range(2):
        both = jnp.concatenate([norms[0][part], norms[1][part]], axis=1).astype(F32)
        aux = jnp.where(arow == part, both, aux)
    aux = aux.astype(BF16)
    for dev in range(SEQ):
        msg[dev, 2 * ROWS : 2 * ROWS + AUX, :] = aux


def gather_kernel(slots, len_ref, rp, m, out, gn, acc, aacc, low):
    ends = ends_of(len_ref)
    acc[...] = jnp.zeros_like(acc)
    aacc[...] = jnp.zeros_like(aacc)
    for dev in range(SEQ):
        for r in range(2):
            p = rp[2 * dev + r, 0]
            acc[p] += m[dev, r * ROWS : (r + 1) * ROWS, :].astype(F32)
            aacc[r, p] += m[dev, 2 * ROWS : 2 * ROWS + AUX, :].astype(F32)
    for p in range(PROMPTS):
        low[p] = acc[p].astype(BF16)
        total = jnp.zeros((1, DK), F32)
        for r in range(2):
            cols = slice(r * DK, (r + 1) * DK)
            total = total + (aacc[r, p, 0:1, cols] + aacc[r, p, 1:2, cols])
        gn[p : p + 1, :] = total.astype(BF16).astype(F32)
    gn[PROMPTS:, :] = jnp.zeros((8 - PROMPTS, DK), F32)
    for dev in range(SEQ):
        first = first_prompt(dev, ends, slots)
        for s in range(slots):
            out[dev, s * ROWS : (s + 1) * ROWS, :] = low[jnp.minimum(first + s, PROMPTS - 1)]


def prompt_kernel(slots, len_ref, m, gn, expo, aft, pk, pv, kg, vg):
    me = lax.axis_index("seq")
    ends = ends_of(len_ref)
    groups = WIN // LANES
    pid = window_pid(me, ends)
    after = jnp.zeros((groups, LANES), F32)
    for p in range(PROMPTS):
        after = jnp.where(pid == p, aft[0:1, p : p + 1], after)
    weight = jnp.exp(expo[...] + after)
    first = first_prompt(me, ends, slots)
    stacked = jnp.concatenate(
        [jnp.where(pid == first + s, weight, 0.0) for s in range(slots)], axis=0
    )
    if slots * groups < LANES:
        stacked = jnp.concatenate(
            [stacked, jnp.zeros((LANES - slots * groups, LANES), F32)], axis=0
        )
    columns = stacked.T
    grads = [m[:, s * ROWS : (s + 1) * ROWS, :].reshape(DK, DV) for s in range(slots)]
    norms = [gn[pl.ds(jnp.minimum(first + s, PROMPTS - 1), 1), :] for s in range(slots)]
    for r in range(groups):
        rows = slice(r * LANES, (r + 1) * LANES)
        keys = pk[rows, :].astype(F32)
        values = pv[rows, :]
        key_grad = jnp.zeros((LANES, DK), F32)
        value_grad = jnp.zeros((LANES, DV), F32)
        for s in range(slots):
            w = columns[:, s * groups + r : s * groups + r + 1]
            value_grad = value_grad + dot((keys * w).astype(BF16), grads[s], 1, 0)
            key_grad = key_grad + w * (dot(values, grads[s], 1, 1) + norms[s])
        kg[rows, :] = key_grad.astype(BF16)
        vg[rows, :] = value_grad.astype(BF16)


def exchange(x, axis):
    return lax.all_to_all(x, axis, 0, 0, tiled=True)


def step(slots, pk, pv, pin, pf, lengths, rp, q, k, v, rin, rf, gain, og):
    groups = WIN // LANES
    part = functools.partial
    msg1, expo = call(
        part(state_kernel, slots),
        [SMEM] + [VMEM] * 4,
        [((SEQ, slots * ROWS + AUX, DV), BF16), ((groups, LANES), F32)],
        [
            pltpu.VMEM((groups, LANES), F32),
            pltpu.VMEM((groups, LANES), F32),
            pltpu.VMEM((slots, WIN, DK), BF16),
        ],
        name="state_kernel",
    )(lengths, pk, pv, pin, pf)
    got1 = exchange(msg1, "seq")
    num, cols = call(
        respond_kernel,
        [VMEM] * 5,
        [((2, RLEN, DV), F32), ((RLEN, LANES), F32)],
        [],
        name="respond_kernel",
    )(q, k, v, rin, rf)
    msg2, aft = call(
        part(spread_kernel, slots),
        [SMEM, SMEM] + [VMEM] * 3,
        [((SEQ, 2 * ROWS + AUX, DV), BF16), ((8, LANES), F32)],
        [
            pltpu.VMEM((PROMPTS + slots, ROWS, DV), F32),
            pltpu.VMEM((PROMPTS, ROWS, DV), BF16),
            pltpu.VMEM((SEQ, LANES), F32),
        ],
        name="spread_kernel",
    )(lengths, rp, got1, expo, pk)
    got2 = exchange(msg2, "seq")
    hid, cols2, msg3 = call(
        hidden_kernel,
        [SMEM] + [VMEM] * 6,
        [((2, RLEN, DV), F32), ((RLEN, LANES), F32), ((HEADS, 8, RLEN), F32)],
        [pltpu.VMEM((8, DK), F32)],
        name="hidden_kernel",
    )(rp, q, got2, num, cols, og, gain)
    got3 = exchange(msg3, "head")
    resp_out, msg4 = call(
        grad_kernel,
        [VMEM] * 6,
        [((2, RLEN, DV), BF16), ((SEQ, 2 * ROWS + AUX, DV), BF16)],
        [],
        name="grad_kernel",
    )(got3, hid, cols2, og, gain, q)
    got4 = exchange(msg4, "seq")
    msg5, gn = call(
        part(gather_kernel, slots),
        [SMEM, SMEM, VMEM],
        [((SEQ, slots * ROWS, DV), BF16), ((8, DK), F32)],
        [
            pltpu.VMEM((PROMPTS, ROWS, DV), F32),
            pltpu.VMEM((2, PROMPTS, AUX, DV), F32),
            pltpu.VMEM((PROMPTS, ROWS, DV), BF16),
        ],
        name="gather_kernel",
    )(lengths, rp, got4)
    got5 = exchange(msg5, "seq")
    key_grad, value_grad = call(
        part(prompt_kernel, slots),
        [SMEM] + [VMEM] * 6,
        [((WIN, DK), BF16), ((WIN, DV), BF16)],
        [],
        name="prompt_kernel",
    )(lengths, got5, gn, expo, aft, pk, pv)
    return resp_out, key_grad, value_grad


def local(pk, pv, pin, pf, lengths, rp, q, k, v, rin, rf, gain, og):
    return step(4, pk, pv, pin, pf, lengths, rp, q, k, v, rin, rf, gain.reshape(1, DV), og)


def solution(mesh):
    in_specs = (
        P("seq", "head"),
        P("seq", "head"),
        P("head", "seq"),
        P("head", "seq"),
        P(),
        P(),
        P("seq", None, "head"),
        P("seq", None, "head"),
        P("seq", None, "head"),
        P("head", "seq", None),
        P("head", "seq", None),
        P("head"),
        P("seq", None, "head"),
    )
    out_specs = (P("seq", None, "head"), P("seq", "head"), P("seq", "head"))
    return jax.shard_map(local, mesh=mesh, in_specs=in_specs, out_specs=out_specs, check_vma=False)
```

time: 283 us -> 114 us (0.40); the launches traced: 280 us -> 114 us
  waiting for transfers between devices: 99.6 us -> 25.2 us
  local copies, waits for them, and re-layouts: 63.6 us -> 8.63 us
  blocking collectives: 9.71 us -> 45.5 us
  other arithmetic: 33.6 us -> 0 us
  Pallas kernels: 0 us -> 21.9 us
  matrix products: 19 us -> 0 us
  loops' own time: 15.8 us -> 0 us
  between operations: 14.5 us -> 0.78 us
  starting transfers between devices: 24 us -> 11.7 us
    all_gather x1 -> x0, waiting for transfers between devices: 38.1 us -> none  [side_by_side(): whole = lax.all_gather(both, axis, axis=dim, tiled=True)]
    all_to_all x5 -> x2, waiting for transfers between devices: 61.5 us -> 25.2 us  [exchange(): return lax.all_to_all(x, axis, 0, 0, tiled=True)]
    all_to_all x1 -> x3, blocking collectives: 9.71 us -> 45.5 us  [exchange(): return lax.all_to_all(x, axis, 0, 0, tiled=True)]
    pallas_call x0 -> x7, Pallas kernels: none -> 21.9 us  [the longest x1 5.74 us: step(): call(part(prompt_kernel, slots), [SMEM] + [VMEM] * 6, [((WIN, DK), BF16),...]
    dot_general x20 -> x0, matrix products: 19 us -> none  [the longest x1 4.13 us: respond(): jnp.dot(queries, state_init, preferred_element_type=jnp.float32)]
    another operation x10 -> x0, loops' own time: 15.8 us -> none  [the longest x4 5.78 us: grad_step(): lax.cond(rows_id[0] == rows_id[-1], grad_single, grad_several, 0)]
    slice x18 -> x0, local copies, waits for them, and re-layouts: 15.6 us -> none  [the longest x4 5.1 us: state_step(): added = lax.cond(rows_id[0] == rows_id[-1], state_single, state_several, 0)]
    squeeze x16 -> x0, local copies, waits for them, and re-layouts: 15.1 us -> none  [local(): lax.scan(state_step, states_init, (weighted_blocks, value_blocks, id_bloc...]
  transfers between devices with their start and end apart: 6 -> 2, of which waited for: 6 -> 2; matrix products, arithmetic and copies ran while one was open for 4% -> 0% of each run, Pallas kernels for 0% -> 2%
where the time goes in v1:
time: 114 us
  blocking collectives  45.5 us (40%)
  waiting for transfers between devices  25.2 us (22%)
  Pallas kernels  21.9 us (19%)
  starting transfers between devices  11.7 us (10%)
  local copies, waits for them, and re-layouts  8.63 us (8%)
    all_to_all x3, blocking collectives, exchange(): return lax.all_to_all(x, axis, 0, 0, tiled=True)  45.5 us
    all_to_all x2, waiting for transfers between devices, exchange(): return lax.all_to_all(x, axis, 0, 0, tiled=True)  25.2 us
    all_to_all x2, starting transfers between devices, exchange(): return lax.all_to_all(x, axis, 0, 0, tiled=True)  11.7 us
    unnamed x39, local copies, waits for them, and re-layouts  8.63 us
    pallas_call x1, Pallas kernels, step(): call(part(prompt_kernel, slots), [SMEM] + [VMEM] * 6, [((WIN, DK), BF16),...  5.74 us
    pallas_call x1, Pallas kernels, step(): call(part(state_kernel, slots), [SMEM] + [VMEM] * 4, [((SEQ, slots * ROWS...  4.29 us
    pallas_call x1, Pallas kernels, step(): call(hidden_kernel, [SMEM] + [VMEM] * 6, [((2, RLEN, DV), F32), ((RLEN, L...  4.07 us
    pallas_call x1, Pallas kernels, step(): call(grad_kernel, [VMEM] * 6, [((2, RLEN, DV), BF16), ((SEQ, 2 * ROWS + A...  2.52 us
  transfers between devices with their start and end apart: 2, of which 2 were waited for; matrix products, arithmetic and copies ran while one was open for 0% of the time, Pallas kernels for 2%

profile of v1, /device:TPU:0, one launch (start us, length us, event | category | flops | bytes accessed | tf_op | source)
XLA Modules:
  0.0 113.7 jit_solution(15162986881321844194)
XLA Ops:
  0.6 0.0 copy-start
  0.6 1.0 copy-done
  1.7 0.0 copy-start.4
  1.7 1.2 %copy-done.4 = bf16[1024,512]{1,0:T(8,128)(2,1)S(1)} copy-done((bf16[1024,512]{1,0:T(8,128)(2,1)S(1)}, bf16[1024,512]{1,0:T(8,128)(2,1)}, u32[]{:S(2)}) %copy-start.4) | copy-done | bytes 1048600
  2.9 0.7 copy-done.12
  3.6 0.0 copy-start.14
  3.6 0.7 copy-done.14
  4.2 0.0 copy-start.15
  4.2 0.7 copy-done.15
  4.9 0.0 copy-start.18
  4.9 0.0 copy-start.1
  4.9 0.0 copy-start.13
  4.9 4.3 %state_kernel.1 = (bf16[16,72,512]{2,1,0:T(8,128)(2,1)}, f32[8,128]{1,0:T(8,128)S(1)}) custom-call(s32[4]{0:T(128)S(1)} %copy-done.12, bf16[1024,256]{1,0:T(8,128)(2,1)S(1)} %copy-done, bf16[1024,512]{1,0:T(8,128)(2,1)S(1)} %copy-done.4, f32[1,1024]{1,0:T(1,128)S(1)} %copy-done.14, f32[1,1024]{1,0:T(1,128)S(1)} %copy-done.15), custom_call_target="tpu_custom_call" | custom-call | tf_op jit(solution)/shard_map/state_kernel/pallas_call | solution.py:374
  9.2 8.0 %all-to-all-start = ((bf16[16,72,512]{2,1,0:T(8,128)(2,1)}), bf16[16,72,512]{2,1,0:T(8,128)(2,1)S(1)}, u32[]{:S(2)}, u32[]{:S(2)}) async-start(bf16[16,72,512]{2,1,0:T(8,128)(2,1)} %get-tuple-element.18), calls=%async_computation | async-start | bytes 2359296 | tf_op jit(solution)/shard_map/all_to_all | solution.py:368
  17.2 0.0 copy-done.18
  17.2 0.0 copy-start.2
  17.2 0.0 copy-start.8
  17.3 0.0 copy-start.16
  17.3 0.0 copy-start.17
  17.3 0.1 copy.17.rp
  17.4 19.2 %all-to-all-done.m = bf16[16,72,512]{2,1,0:T(8,128)(2,1)S(1)} async-done(((bf16[16,72,512]{2,1,0:T(8,128)(2,1)}), bf16[16,72,512]{2,1,0:T(8,128)(2,1)S(1)}, u32[]{:S(2)}, u32[]{:S(2)}) %all-to-all-start) | async-done | bytes 1179680 | tf_op jit(solution)/shard_map/all_to_all | solution.py:368
  36.5 0.0 copy-done.1
  36.5 0.0 copy-done.13
  36.5 2.4 %spread_kernel.1 = (bf16[16,40,512]{2,1,0:T(8,128)(2,1)}, f32[8,128]{1,0:T(8,128)S(1)}) custom-call(s32[4]{0:T(128)S(1)} %copy-done.13, s32[32,1]{1,0:T(8,128)S(1)} %copy.17.rp, bf16[16,72,512]{2,1,0:T(8,128)(2,1)S(1)} %all-to-all-done.m, f32[8,128]{1,0:T(8,128)S(1)} %get-tuple-element.19.expo, bf16[1024,256]{1,0:T(8,128)(2,1)S(1)} %copy-done.1), custom_call_target="tpu_custom_call" | custom-call | tf_op jit(solution)/shard_map/spread_kernel/pallas_call | solution.py:393
  38.9 0.0 copy-start.3
  38.9 3.7 %all-to-all-start.1 = ((bf16[16,40,512]{2,1,0:T(8,128)(2,1)}), bf16[16,40,512]{2,1,0:T(8,128)(2,1)S(1)}, u32[]{:S(2)}, u32[]{:S(2)}) async-start(bf16[16,40,512]{2,1,0:T(8,128)(2,1)} %get-tuple-element.20), calls=%async_computation.1 | async-start | bytes 1310720 | tf_op jit(solution)/shard_map/all_to_all | solution.py:368
  42.6 0.0 copy-done.2
  42.6 0.0 copy-done.8
  42.7 0.0 copy-done.16
  42.7 0.0 copy-done.17
  42.7 0.0 copy-start.7
  42.7 1.2 %copy-done.7 = bf16[2,512,512]{2,1,0:T(8,128)(2,1)S(1)} copy-done((bf16[2,512,512]{2,1,0:T(8,128)(2,1)S(1)}, bf16[2,512,512]{2,1,0:T(8,128)(2,1)}, u32[]{:S(2)}) %copy-start.7) | copy-done | bytes 1048600
  43.9 1.8 %respond_kernel.1 = (f32[2,512,512]{2,1,0:T(8,128)S(1)}, f32[512,128]{1,0:T(8,128)S(1)}) custom-call(bf16[2,512,256]{2,1,0:T(8,128)(2,1)S(1)} %copy-done.2, bf16[2,512,256]{2,1,0:T(8,128)(2,1)S(1)} %copy-done.8, bf16[2,512,512]{2,1,0:T(8,128)(2,1)S(1)} %copy-done.7, f32[1,2,512]{2,1,0:T(2,128)S(1)} %copy-done.16, f32[1,2,512]{2,1,0:T(2,128)S(1)} %copy-done.17), custom_call_target="tpu_custom_call" | custom-call | tf_op jit(solution)/shard_map/respond_kernel/pallas_call | solution.py:386
  45.7 0.0 copy-start.6
  45.7 1.3 %copy-done.6 = f32[2,512,512]{2,1,0:T(8,128)} copy-done((f32[2,512,512]{2,1,0:T(8,128)}, f32[2,512,512]{2,1,0:T(8,128)S(1)}, u32[]{:S(2)}) %copy-start.6) | copy-done | bytes 2097176
  47.0 0.7 copy-done.9
  47.7 6.0 %all-to-all-done.1.m = bf16[16,40,512]{2,1,0:T(8,128)(2,1)S(1)} async-done(((bf16[16,40,512]{2,1,0:T(8,128)(2,1)}), bf16[16,40,512]{2,1,0:T(8,128)(2,1)S(1)}, u32[]{:S(2)}, u32[]{:S(2)}) %all-to-all-start.1) | async-done | bytes 655392 | tf_op jit(solution)/shard_map/all_to_all | solution.py:368
  53.8 0.0 copy-done.3
  53.8 0.0 copy-done.11
  53.8 0.9 copy-done.10
  54.7 4.1 %hidden_kernel.1 = (f32[2,512,512]{2,1,0:T(8,128)S(1)}, f32[512,128]{1,0:T(8,128)S(1)}, f32[8,8,512]{2,1,0:T(8,128)S(1)}) custom-call(s32[32,1]{1,0:T(8,128)S(1)} %copy.17.rp, bf16[2,512,256]{2,1,0:T(8,128)(2,1)S(1)} %copy-done.2, bf16[16,40,512]{2,1,0:T(8,128)(2,1)S(1)} %all-to-all-done.1.m, f32[2,512,512]{2,1,0:T(8,128)} %copy-done.6, ...), custom_call_target="tpu_custom_call" | custom-call | tf_op jit(solution)/shard_map/hidden_kernel/pallas_call | solution.py:405
  58.8 10.4 %all_to_all.25.m = f32[8,8,512]{2,1,0:T(8,128)S(1)} all-to-all(f32[8,8,512]{2,1,0:T(8,128)S(1)} %get-tuple-element.23), channel_id=1, replica_groups=mesh['seq'=16,'head'=8] {'head'}, dimensions={0} | all-to-all | bytes 262144 | tf_op jit(solution)/shard_map/all_to_all | solution.py:368
  69.2 2.5 %grad_kernel.1 = (bf16[2,512,512]{2,1,0:T(8,128)(2,1)}, bf16[16,40,512]{2,1,0:T(8,128)(2,1)S(1)}) custom-call(f32[8,8,512]{2,1,0:T(8,128)S(1)} %all_to_all.25.m, f32[2,512,512]{2,1,0:T(8,128)S(1)} %get-tuple-element.24.hid, f32[512,128]{1,0:T(8,128)S(1)} %get-tuple-element.25.cols2, bf16[2,512,512]{2,1,0:T(8,128)(2,1)S(1)} %copy-done.3, ...), custom_call_target="tpu_custom_call" | custom-call | tf_op jit(solution)/shard_map/grad_kernel/pallas_call | solution.py:413
  71.7 15.9 %all_to_all.26.m = bf16[16,40,512]{2,1,0:T(8,128)(2,1)S(1)} all-to-all(bf16[16,40,512]{2,1,0:T(8,128)(2,1)S(1)} %get-tuple-element.27), channel_id=1, replica_groups=mesh['seq'=16,'head'=8] {'seq'}, dimensions={0} | all-to-all | bytes 1310720 | tf_op jit(solution)/shard_map/all_to_all | solution.py:368
  87.6 1.1 gather_kernel.1
  88.7 19.2 %all_to_all.27.m = bf16[16,64,512]{2,1,0:T(8,128)(2,1)S(1)} all-to-all(bf16[16,64,512]{2,1,0:T(8,128)(2,1)S(1)} %get-tuple-element.28), channel_id=1, replica_groups=mesh['seq'=16,'head'=8] {'seq'}, dimensions={0} | all-to-all | bytes 2097152 | tf_op jit(solution)/shard_map/all_to_all | solution.py:368
  108.0 0.0 copy-done.5
  108.0 5.7 %prompt_kernel.1 = (bf16[1024,256]{1,0:T(8,128)(2,1)}, bf16[1024,512]{1,0:T(8,128)(2,1)}) custom-call(s32[4]{0:T(128)S(1)} %copy-done.13, bf16[16,64,512]{2,1,0:T(8,128)(2,1)S(1)} %all_to_all.27.m, f32[8,256]{1,0:T(8,128)S(1)} %get-tuple-element.29.gn, f32[8,128]{1,0:T(8,128)S(1)} %get-tuple-element.19.expo, f32[8,128]{1,0:T(8,128)S(1)} %get-tuple-element.30.aft, ...), custom_call_target="tpu_custom_call" | custom-call | tf_op jit(solution)/shard_map/prompt_kernel/pallas_call | solution.py:433
  (5 shorter events, 0.0 us)
Async XLA Ops:
  0.6 1.0 copy-start
  1.7 1.2 %copy-start.4 = (bf16[1024,512]{1,0:T(8,128)(2,1)S(1)}, bf16[1024,512]{1,0:T(8,128)(2,1)}, u32[]{:S(2)}) copy-start(bf16[1024,512]{1,0:T(8,128)(2,1)} %pv.3) | copy-start | bytes 3145732
  2.9 0.7 copy-start.12
  3.6 0.7 copy-start.14
  4.2 0.7 copy-start.15
  4.9 12.3 %copy-start.18 = (s32[32,1]{0,1:T(1,128)S(1)}, s32[32,1]{0,1:T(1,128)}, u32[]{:S(2)}) copy-start(s32[32,1]{0,1:T(1,128)} %param.18) | copy-start | bytes 388
  4.9 31.6 %copy-start.1 = (bf16[1024,256]{1,0:T(8,128)(2,1)S(1)}, bf16[1024,256]{1,0:T(8,128)(2,1)}, u32[]{:S(2)}) copy-start(bf16[1024,256]{1,0:T(8,128)(2,1)} %pk.5) | copy-start | bytes 1572868
  4.9 31.6 %copy-start.13 = (s32[4]{0:T(128)S(1)}, s32[4]{0:T(128)}, u32[]{:S(2)}) copy-start(s32[4]{0:T(128)} %len_ref.7) | copy-start | bytes 52
  9.2 27.3 %all-to-all-start = ((bf16[16,72,512]{2,1,0:T(8,128)(2,1)}), bf16[16,72,512]{2,1,0:T(8,128)(2,1)S(1)}, u32[]{:S(2)}, u32[]{:S(2)}) async-start(bf16[16,72,512]{2,1,0:T(8,128)(2,1)} %get-tuple-element.18), calls=%async_computation | async-start | bytes 2359296 | tf_op jit(solution)/shard_map/all_to_all | solution.py:368
  17.2 25.4 %copy-start.2 = (bf16[2,512,256]{2,1,0:T(8,128)(2,1)S(1)}, bf16[2,512,256]{2,1,0:T(8,128)(2,1)}, u32[]{:S(2)}) copy-start(bf16[2,512,256]{2,1,0:T(8,128)(2,1)} %q.5) | copy-start | bytes 1572868
  17.2 25.4 %copy-start.8 = (bf16[2,512,256]{2,1,0:T(8,128)(2,1)S(1)}, bf16[2,512,256]{2,1,0:T(8,128)(2,1)}, u32[]{:S(2)}) copy-start(bf16[2,512,256]{2,1,0:T(8,128)(2,1)} %k.1) | copy-start | bytes 1572868
  17.3 25.4 %copy-start.16 = (f32[1,2,512]{2,1,0:T(2,128)S(1)}, f32[1,2,512]{2,1,0:T(2,128)}, u32[]{:S(2)}) copy-start(f32[1,2,512]{2,1,0:T(2,128)} %rin.1) | copy-start | bytes 12292
  17.3 25.4 %copy-start.17 = (f32[1,2,512]{2,1,0:T(2,128)S(1)}, f32[1,2,512]{2,1,0:T(2,128)}, u32[]{:S(2)}) copy-start(f32[1,2,512]{2,1,0:T(2,128)} %rf.1) | copy-start | bytes 12292
  38.9 14.9 %copy-start.3 = (bf16[2,512,512]{2,1,0:T(8,128)(2,1)S(1)}, bf16[2,512,512]{2,1,0:T(8,128)(2,1)}, u32[]{:S(2)}) copy-start(bf16[2,512,512]{2,1,0:T(8,128)(2,1)} %og.3) | copy-start | bytes 3145732
  38.9 14.9 %copy-start.11 = (f32[512]{0:T(512)S(1)}, f32[512]{0:T(512)}, u32[]{:S(2)}) copy-start(f32[512]{0:T(512)} %param.24) | copy-start | bytes 6148
  38.9 14.9 %all-to-all-start.1 = ((bf16[16,40,512]{2,1,0:T(8,128)(2,1)}), bf16[16,40,512]{2,1,0:T(8,128)(2,1)S(1)}, u32[]{:S(2)}, u32[]{:S(2)}) async-start(bf16[16,40,512]{2,1,0:T(8,128)(2,1)} %get-tuple-element.20), calls=%async_computation.1 | async-start | bytes 1310720 | tf_op jit(solution)/shard_map/all_to_all | solution.py:368
  42.7 1.2 %copy-start.7 = (bf16[2,512,512]{2,1,0:T(8,128)(2,1)S(1)}, bf16[2,512,512]{2,1,0:T(8,128)(2,1)}, u32[]{:S(2)}) copy-start(bf16[2,512,512]{2,1,0:T(8,128)(2,1)} %v.1) | copy-start | bytes 3145732
  45.7 1.3 %copy-start.6 = (f32[2,512,512]{2,1,0:T(8,128)}, f32[2,512,512]{2,1,0:T(8,128)S(1)}, u32[]{:S(2)}) copy-start(f32[2,512,512]{2,1,0:T(8,128)S(1)} %get-tuple-element.21.num) | copy-start | bytes 6291460
  47.0 0.7 copy-start.9
  53.8 1.0 copy-start.10
  71.7 36.3 %copy-start.5 = (bf16[1024,512]{1,0:T(8,128)(2,1)S(1)}, bf16[1024,512]{1,0:T(8,128)(2,1)}, u32[]{:S(2)}) copy-start(bf16[1024,512]{1,0:T(8,128)(2,1)} %pv.3) | copy-start | bytes 3145732

commit v2 on v1

v2 whole, which is shorter than its diff:
```python
import functools

import jax
import jax.numpy as jnp
from jax import lax
from jax.experimental import pallas as pl
from jax.experimental.pallas import tpu as pltpu
from jax.sharding import PartitionSpec as P

F32 = jnp.float32
BF16 = jnp.bfloat16
PROMPTS = 4
SEQ = 16
HEADS = 8
DK = 256
DV = 512
WIN = 1024
RLEN = 512
ROWS = DK // SEQ
LANES = 128
TILES = DV // LANES
STATE = ROWS * TILES
AUX = 8
NAUX = 16
GROUP = 256
SCALE = DK ** (-0.5)

VMEM = pl.BlockSpec(memory_space=pltpu.VMEM)
SMEM = pl.BlockSpec(memory_space=pltpu.SMEM)
HBM = pl.BlockSpec(memory_space=pltpu.HBM)
ANY = pl.BlockSpec(memory_space=pl.ANY)


def call(body, ins, outs, scratch, spec=VMEM, **kw):
    return pl.pallas_call(
        body,
        in_specs=ins,
        out_specs=tuple(spec for _ in outs),
        out_shape=tuple(jax.ShapeDtypeStruct(s, d) for s, d in outs),
        scratch_shapes=scratch,
        compiler_params=pltpu.CompilerParams(vmem_limit_bytes=24 << 20),
        **kw,
    )


def iota(shape, dim):
    return lax.broadcasted_iota(jnp.int32, shape, dim)


def ends_of(len_ref):
    e0 = len_ref[0]
    e1 = e0 + len_ref[1]
    e2 = e1 + len_ref[2]
    return e0, e1, e2


def prompt_at(position, ends):
    total = 0
    for e in ends:
        total = total + (position >= e).astype(jnp.int32)
    return total


def first_prompt(device, ends, slots):
    if slots == PROMPTS:
        return 0
    total = jnp.int32(0)
    for e in ends:
        total = total + jnp.where(device * WIN >= e, 1, 0)
    return total


def log_sigmoid(x):
    return jnp.minimum(x, 0.0) - jnp.log1p(jnp.exp(-jnp.abs(x)))


def dot(a, b, ca, cb):
    return lax.dot_general(a, b, (((ca,), (cb,)), ((), ())), preferred_element_type=F32)


def split_two(x):
    hi = x.astype(BF16)
    return hi, (x - hi.astype(F32)).astype(BF16)


def send_state(msg, dev, slot, rows):
    for c in range(TILES):
        at = slot * STATE + c * ROWS
        msg[dev, at : at + ROWS, :] = rows[:, c * LANES : (c + 1) * LANES]


def received(m, slot):
    tiles = []
    for c in range(TILES):
        start = slot * STATE + c * ROWS
        if not isinstance(start, int):
            start = pl.multiple_of(start, ROWS)
        tiles.append(m[:, pl.ds(start, ROWS), :].reshape(DK, LANES))
    return jnp.concatenate(tiles, axis=1)


def whole(x):
    return jnp.sum(jnp.sum(x, axis=0, keepdims=True), axis=1, keepdims=True)


def window_pid(me, ends):
    shape = (WIN // LANES, LANES)
    return prompt_at(me * WIN + iota(shape, 0) * LANES + iota(shape, 1), ends)


def state_kernel(
    slots, len_hbm, pk_hbm, pv_hbm, pin_hbm, pf_hbm, msg, e_out, len_ref, gates, inputs, pk, pv, wmat, sems
):
    me = lax.axis_index("seq")
    groups = WIN // LANES
    copies = [
        pltpu.make_async_copy(len_hbm, len_ref, sems.at[0]),
        pltpu.make_async_copy(pf_hbm, gates, sems.at[1]),
        pltpu.make_async_copy(pin_hbm, inputs, sems.at[2]),
        pltpu.make_async_copy(pk_hbm, pk, sems.at[3]),
        pltpu.make_async_copy(pv_hbm, pv, sems.at[4]),
    ]
    for copy in copies:
        copy.start()
    for copy in copies[:3]:
        copy.wait()
    ends = ends_of(len_ref)
    shape = (groups, LANES)
    pid = window_pid(me, ends)
    lane, row = iota(shape, 1), iota(shape, 0)

    def folded(ref):
        return jnp.concatenate(
            [ref[:, r * LANES : (r + 1) * LANES] for r in range(groups)], axis=0
        )

    lf = log_sigmoid(folded(gates))
    tail = lf
    step = 1
    while step < LANES:
        tail = tail + jnp.where(lane < LANES - step, pltpu.roll(tail, LANES - step, 1), 0.0)
        step *= 2
    after = jnp.broadcast_to(tail[:, 0:1], shape)
    after = jnp.where(row < groups - 1, pltpu.roll(after, groups - 1, 0), 0.0)
    step = 1
    while step < groups:
        after = after + jnp.where(row < groups - step, pltpu.roll(after, groups - step, 0), 0.0)
        step *= 2
    sums = [whole(jnp.where(pid == p, lf, 0.0)) for p in range(PROMPTS)]
    later = jnp.where(
        pid == 0,
        sums[1] + sums[2] + sums[3],
        jnp.where(pid == 1, sums[2] + sums[3], jnp.where(pid == 2, sums[3], 0.0)),
    )
    expo = folded(inputs) + ((tail - lf) + after - later)
    e_out[...] = expo
    weight = jnp.exp(expo)
    first = first_prompt(me, ends, slots)
    stacked = jnp.concatenate(
        [jnp.where(pid == first + s, weight, 0.0) for s in range(slots)]
        + [jnp.zeros((LANES - slots * groups, LANES), F32)],
        axis=0,
    )
    columns = stacked.T
    ashape = (AUX, LANES)
    arow, alane = iota(ashape, 0), iota(ashape, 1)
    aux = jnp.zeros(ashape, F32)
    for p in range(PROMPTS):
        rest = jnp.broadcast_to(sums[p], ashape)
        for part in range(3):
            piece = rest.astype(BF16).astype(F32)
            aux = jnp.where((arow == part) & (alane == p), piece, aux)
            rest = rest - piece
    aux = aux.astype(BF16)
    for dev in range(SEQ):
        msg[dev, slots * STATE : slots * STATE + AUX, :] = aux
    copies[3].wait()
    for r in range(groups):
        rows = slice(r * LANES, (r + 1) * LANES)
        keys = pk[rows, :].astype(F32)
        for s in range(slots):
            at = s * groups + r
            wmat[s, rows, :] = (keys * columns[:, at : at + 1]).astype(BF16)
    copies[4].wait()
    for s in range(slots):
        state = dot(wmat[s], pv[...], 0, 0).astype(BF16)
        for dev in range(SEQ):
            send_state(msg, dev, s, state[dev * ROWS : (dev + 1) * ROWS, :])


def spread_kernel(slots, len_ref, rp, m, expo, pk, unused, out, aft, acc, low, afters):
    me = lax.axis_index("seq")
    ends = ends_of(len_ref)
    shape = (SEQ, LANES)
    lane, row = iota(shape, 1), iota(shape, 0)
    base = slots * STATE
    gates = m[:, base : base + AUX, :].astype(F32)
    sums = gates[:, 2, :] + gates[:, 1, :] + gates[:, 0, :]
    after = jnp.where(row < SEQ - 1, pltpu.roll(sums, SEQ - 1, 0), 0.0)
    step = 1
    while step < SEQ:
        after = after + jnp.where(row < SEQ - step, pltpu.roll(after, SEQ - step, 0), 0.0)
        step *= 2
    afters[...] = after
    mine = jnp.broadcast_to(afters[pl.ds(me, 1), :], aft.shape)
    aft[...] = mine
    factor = jnp.exp(after)
    if slots == PROMPTS:
        first = jnp.zeros(shape, jnp.int32)
    else:
        first = prompt_at(row * WIN, ends)
    acc[...] = jnp.zeros_like(acc)
    for s in range(slots):
        scale = jnp.sum(jnp.where(lane == first + s, factor, 0.0), axis=1, keepdims=True)
        for dev in range(SEQ):
            p = first_prompt(dev, ends, slots) + s
            f = scale[dev : dev + 1, :]
            acc[p] += f * m[dev, s * STATE : (s + 1) * STATE, :].astype(F32)
    for p in range(PROMPTS):
        low[p] = acc[p].astype(BF16)
    groups = WIN // LANES
    pid = window_pid(me, ends)
    rest = jnp.zeros((groups, LANES), F32)
    for p in range(PROMPTS):
        rest = jnp.where(pid == p, mine[0:1, p : p + 1], rest)
    weight = jnp.exp(expo[...] + rest)
    columns = jnp.concatenate([weight, jnp.zeros((LANES - groups, LANES), F32)], axis=0).T
    mrow = iota((8, LANES), 0)
    norms = jnp.zeros((8, DK), F32)
    for r in range(groups):
        weighted = pk[r * LANES : (r + 1) * LANES, :].astype(F32) * columns[:, r : r + 1]
        member = (jnp.broadcast_to(pid[r : r + 1, :], (8, LANES)) == mrow).astype(F32)
        norms = norms + dot(member.astype(BF16), weighted.astype(BF16), 1, 0)
    aux = []
    for piece in split_two(norms):
        piece = piece.astype(F32)
        aux += [piece[0:PROMPTS, 0:LANES], piece[0:PROMPTS, LANES:DK]]
    aux = jnp.concatenate(aux, axis=0).astype(BF16)
    for dev in range(SEQ):
        for r in range(2):
            out[dev, r * STATE : (r + 1) * STATE, :] = low[rp[2 * dev + r, 0]]
        out[dev, 2 * STATE : 2 * STATE + NAUX, :] = aux


def respond_kernel(q, k, v, rin, rf, num, cols):
    shape = (8, RLEN)
    row, lane = iota(shape, 0), iota(shape, 1)
    gate = jnp.where(row == 0, rf[0, 0:1, :], rf[0, 1:2, :])
    cum = log_sigmoid(gate)
    step = 1
    while step < RLEN:
        cum = cum + jnp.where(lane >= step, pltpu.roll(cum, step, 1), 0.0)
        step *= 2
    tall = jnp.concatenate([cum, jnp.zeros((LANES - 8, RLEN), F32)], axis=0).T
    half = RLEN // 2
    clane = iota((RLEN, LANES), 1)
    packed = jnp.zeros((RLEN, LANES), F32)
    for r in range(2):
        ccol = tall[:, r : r + 1]
        srow = rin[0, r : r + 1, :] - cum[r : r + 1, :]
        for b in range(2):
            rows = slice(b * half, (b + 1) * half)
            width = (b + 1) * half
            scores = dot(q[r, rows, :], k[r, 0:width, :], 1, 1) * SCALE
            causal = iota((half, width), 0) + b * half >= iota((half, width), 1)
            decay = jnp.where(causal, ccol[rows, :] + srow[:, 0:width], -1e30)
            mixing = (scores * jnp.exp(decay)).astype(BF16)
            num[r, rows, :] = dot(mixing, v[r, 0:width, :], 1, 0)
            den = jnp.sum(mixing.astype(F32), axis=1, keepdims=True)
            cols[rows, :] = jnp.where(
                clane[rows, :] == r, den, packed[rows, :] if r == 0 else cols[rows, :]
            )
        lifted = jnp.exp(ccol) * SCALE
        cols[...] = jnp.where(clane == 2 + r, lifted, cols[...])


def hidden_kernel(rp, q, m, num, cols, og, gain, hid, cols2, msg, nrm):
    me = lax.axis_index("seq")
    aux = jnp.sum(m[:, 2 * STATE : 2 * STATE + NAUX, :].astype(F32), axis=0)
    aux = aux[0:8, :] + aux[8:16, :]
    nrm[0:PROMPTS, :] = jnp.concatenate([aux[0:PROMPTS, :], aux[PROMPTS:8, :]], axis=1)
    clane = iota((RLEN, LANES), 1)
    sums = jnp.zeros((RLEN, LANES), F32)
    packed = jnp.zeros((RLEN, LANES), F32)
    for r in range(2):
        norm = jnp.broadcast_to(nrm[pl.ds(rp[2 * me + r, 0], 1), :], (LANES, DK)).astype(BF16)
        lifted = cols[:, 2 + r : 3 + r]
        qn = dot(q[r], norm, 1, 1)[:, 0:1]
        den = cols[:, r : r + 1] + lifted * qn
        inverse = lax.rsqrt(den * den + 1.0)
        hidden = (num[r] + lifted * dot(q[r], received(m, r), 1, 0)) * inverse
        hid[r] = hidden
        squares = jnp.sum(hidden * hidden, axis=1, keepdims=True)
        dots = jnp.sum(og[r].astype(F32) * gain[...] * hidden, axis=1, keepdims=True)
        sums = jnp.where(clane == 2 * r, squares, jnp.where(clane == 2 * r + 1, dots, sums))
        lift = lifted * inverse
        ratio = lifted * den * (inverse * inverse)
        packed = jnp.where(clane == 4 + r, lift, jnp.where(clane == 6 + r, ratio, packed))
    cols2[...] = packed + sums
    rows = sums.T
    rows = jnp.concatenate(
        [rows[0:4, c * LANES : (c + 1) * LANES] for c in range(RLEN // LANES)], axis=0
    )
    for dev in range(HEADS):
        msg[dev] = rows


def grad_kernel(m, hid, cols2, og, gain, q, out, msg, numer, denom):
    total = m[0]
    for dev in range(1, HEADS):
        total = total + m[dev]
    features = HEADS * DV
    total = jnp.concatenate([total, jnp.zeros((LANES - 16, LANES), F32)], axis=0).T
    inverses = lax.rsqrt(total / features + 1e-6)
    coefs = pltpu.roll(total, LANES - 1, 1) * (inverses * inverses * inverses) / features
    rows8 = []
    for r in range(2):
        for c in range(RLEN // LANES):
            rows = slice(c * LANES, (c + 1) * LANES)
            at = 4 * c + 2 * r
            inv, coef = inverses[:, at : at + 1], coefs[:, at : at + 1]
            small = cols2[rows, :]
            squares, dots = small[:, 2 * r : 2 * r + 1], small[:, 2 * r + 1 : 2 * r + 2]
            lift, ratio = small[:, 4 + r : 5 + r], small[:, 6 + r : 7 + r]
            hidden = hid[r, rows, :]
            scaled = gain[...] * inv
            out[r, rows, :] = (hidden * scaled).astype(BF16)
            d_hidden = scaled * og[r, rows, :].astype(F32) - hidden * coef
            numer[rows, :] = (lift * d_hidden).astype(BF16)
            lift_denom = (-(inv * dots - coef * squares) * ratio).astype(BF16).astype(F32)
            part = jnp.sum(lift_denom * q[r, rows, :].astype(F32), axis=0, keepdims=True)
            denom[...] = part if c == 0 else denom[...] + part
        state = dot(q[r], numer[...], 0, 0).astype(BF16)
        for dev in range(SEQ):
            send_state(msg, dev, r, state[dev * ROWS : (dev + 1) * ROWS, :])
        for piece in split_two(denom[...]):
            piece = piece.astype(F32)
            rows8 += [piece[:, 0:LANES], piece[:, LANES:DK]]
    aux = jnp.concatenate(rows8, axis=0).astype(BF16)
    for dev in range(SEQ):
        msg[dev, 2 * STATE : 2 * STATE + AUX, :] = aux


def gather_kernel(slots, len_ref, rp, m, out, gn, acc, aacc, low):
    ends = ends_of(len_ref)
    acc[...] = jnp.zeros_like(acc)
    aacc[...] = jnp.zeros_like(aacc)
    for dev in range(SEQ):
        for r in range(2):
            p = rp[2 * dev + r, 0]
            acc[p] += m[dev, r * STATE : (r + 1) * STATE, :].astype(F32)
            aacc[r, p] += m[dev, 2 * STATE : 2 * STATE + AUX, :].astype(F32)
    for p in range(PROMPTS):
        low[p] = acc[p].astype(BF16)
        total = jnp.zeros((2, LANES), F32)
        for r in range(2):
            total = total + (aacc[r, p, 4 * r : 4 * r + 2, :] + aacc[r, p, 4 * r + 2 : 4 * r + 4, :])
        total = total.astype(BF16).astype(F32)
        gn[p : p + 1, :] = jnp.concatenate([total[0:1, :], total[1:2, :]], axis=1)
    gn[PROMPTS:, :] = jnp.zeros((8 - PROMPTS, DK), F32)
    for dev in range(SEQ):
        first = first_prompt(dev, ends, slots)
        for s in range(slots):
            out[dev, s * STATE : (s + 1) * STATE, :] = low[jnp.minimum(first + s, PROMPTS - 1)]


def prompt_kernel(slots, len_ref, m, gn, expo, aft, pk, pv, kg_hbm, vg_hbm, kg, vg, sems):
    me = lax.axis_index("seq")
    ends = ends_of(len_ref)
    groups = WIN // LANES
    pid = window_pid(me, ends)
    after = jnp.zeros((groups, LANES), F32)
    for p in range(PROMPTS):
        after = jnp.where(pid == p, aft[0:1, p : p + 1], after)
    weight = jnp.exp(expo[...] + after)
    first = first_prompt(me, ends, slots)
    stacked = jnp.concatenate(
        [weight, pid.astype(F32), jnp.zeros((LANES - 2 * groups, LANES), F32)], axis=0
    )
    columns = stacked.T

    def at_row(j):
        total = jnp.int32(0)
        for e in ends:
            total = total + jnp.where(me * WIN + j >= e, 1, 0)
        return total

    copies = []
    per = GROUP // LANES
    for g in range(WIN // GROUP):
        rows = slice(g * GROUP, (g + 1) * GROUP)
        w, ids = (
            jnp.concatenate(
                [columns[:, at + g * per + i : at + g * per + i + 1] for i in range(per)], axis=0
            )
            for at in (0, groups)
        )
        weighted = (pk[rows, :].astype(F32) * w).astype(BF16)
        low, high = at_row(g * GROUP), at_row((g + 1) * GROUP - 1)

        def grads(p):
            grad = received(m, p - first)
            value_grad = dot(weighted, grad, 1, 0)
            key_grad = w * (dot(pv[rows, :], grad, 1, 1) + gn[pl.ds(p, 1), :])
            return key_grad.astype(BF16), value_grad.astype(BF16)

        kg[rows, :], vg[rows, :] = grads(low)

        @pl.loop(low + 1, high + 1)
        def _(p):
            key_grad, value_grad = grads(p)
            mine = ids == p.astype(F32)
            kg[rows, :] = jnp.where(mine, key_grad, kg[rows, :])
            vg[rows, :] = jnp.where(mine, value_grad, vg[rows, :])

        copies += [
            pltpu.make_async_copy(kg.at[rows], kg_hbm.at[rows], sems.at[2 * g]),
            pltpu.make_async_copy(vg.at[rows], vg_hbm.at[rows], sems.at[2 * g + 1]),
        ]
        for copy in copies[-2:]:
            copy.start()
    for copy in copies:
        copy.wait()


def exchange(x, axis):
    return lax.all_to_all(x, axis, 0, 0, tiled=True)


def step(slots, pk, pv, pin, pf, lengths, rp, q, k, v, rin, rf, gain, og):
    groups = WIN // LANES
    part = functools.partial
    msg1, expo = call(
        part(state_kernel, slots),
        [HBM] * 5,
        [((SEQ, slots * STATE + AUX, LANES), BF16), ((groups, LANES), F32)],
        [
            pltpu.SMEM((PROMPTS,), jnp.int32),
            pltpu.VMEM((1, WIN), F32),
            pltpu.VMEM((1, WIN), F32),
            pltpu.VMEM((WIN, DK), BF16),
            pltpu.VMEM((WIN, DV), BF16),
            pltpu.VMEM((slots, WIN, DK), BF16),
            pltpu.SemaphoreType.DMA((5,)),
        ],
        name="state_kernel",
    )(lengths, pk, pv, pin, pf)
    got1 = exchange(msg1, "seq")
    num, cols = call(
        respond_kernel,
        [VMEM] * 5,
        [((2, RLEN, DV), F32), ((RLEN, LANES), F32)],
        [],
        name="respond_kernel",
    )(q, k, v, rin, rf)
    msg2, aft = call(
        part(spread_kernel, slots),
        [SMEM, SMEM] + [VMEM] * 3 + [ANY],
        [((SEQ, 2 * STATE + NAUX, LANES), BF16), ((8, LANES), F32)],
        [
            pltpu.VMEM((PROMPTS + slots, STATE, LANES), F32),
            pltpu.VMEM((PROMPTS, STATE, LANES), BF16),
            pltpu.VMEM((SEQ, LANES), F32),
        ],
        name="spread_kernel",
    )(lengths, rp, got1, expo, pk, cols)
    got2 = exchange(msg2, "seq")
    hid, cols2, msg3 = call(
        hidden_kernel,
        [SMEM] + [VMEM] * 6,
        [((2, RLEN, DV), F32), ((RLEN, LANES), F32), ((HEADS, 16, LANES), F32)],
        [pltpu.VMEM((8, DK), F32)],
        name="hidden_kernel",
    )(rp, q, got2, num, cols, og, gain)
    got3 = exchange(msg3, "head")
    resp_out, msg4 = call(
        grad_kernel,
        [VMEM] * 6,
        [((2, RLEN, DV), BF16), ((SEQ, 2 * STATE + AUX, LANES), BF16)],
        [pltpu.VMEM((RLEN, DV), BF16), pltpu.VMEM((1, DK), F32)],
        name="grad_kernel",
    )(got3, hid, cols2, og, gain, q)
    got4 = exchange(msg4, "seq")
    msg5, gn = call(
        part(gather_kernel, slots),
        [SMEM, SMEM, VMEM],
        [((SEQ, slots * STATE, LANES), BF16), ((8, DK), F32)],
        [
            pltpu.VMEM((PROMPTS, STATE, LANES), F32),
            pltpu.VMEM((2, PROMPTS, AUX, LANES), F32),
            pltpu.VMEM((PROMPTS, STATE, LANES), BF16),
        ],
        name="gather_kernel",
    )(lengths, rp, got4)
    got5 = exchange(msg5, "seq")
    key_grad, value_grad = call(
        part(prompt_kernel, slots),
        [SMEM] + [VMEM] * 6,
        [((WIN, DK), BF16), ((WIN, DV), BF16)],
        [
            pltpu.VMEM((WIN, DK), BF16),
            pltpu.VMEM((WIN, DV), BF16),
            pltpu.SemaphoreType.DMA((2 * WIN // GROUP,)),
        ],
        spec=HBM,
        name="prompt_kernel",
    )(lengths, got5, gn, expo, aft, pk, pv)
    return resp_out, key_grad, value_grad


def local(pk, pv, pin, pf, lengths, rp, q, k, v, rin, rf, gain, og):
    e0 = lengths[0]
    e1 = e0 + lengths[1]
    e2 = e1 + lengths[2]
    crowded = ((e0 // WIN == e1 // WIN) & (e0 % WIN != 0)) | ((e1 // WIN == e2 // WIN) & (e1 % WIN != 0))
    args = (pk, pv, pin, pf, lengths, rp, q, k, v, rin, rf, gain.reshape(1, DV), og)
    return lax.cond(
        crowded, functools.partial(step, PROMPTS), functools.partial(step, 2), *args
    )


def solution(mesh):
    in_specs = (
        P("seq", "head"),
        P("seq", "head"),
        P("head", "seq"),
        P("head", "seq"),
        P(),
        P(),
        P("seq", None, "head"),
        P("seq", None, "head"),
        P("seq", None, "head"),
        P("head", "seq", None),
        P("head", "seq", None),
        P("head"),
        P("seq", None, "head"),
    )
    out_specs = (P("seq", None, "head"), P("seq", "head"), P("seq", "head"))
    return jax.shard_map(local, mesh=mesh, in_specs=in_specs, out_specs=out_specs, check_vma=False)
```

time: 114 us -> 95.4 us (0.84)
  waiting for transfers between devices: 25.2 us -> 8.42 us
  blocking collectives: 45.5 us -> 52.9 us
  local copies, waits for them, and re-layouts: 8.63 us -> 1.49 us
  between operations: 0.78 us -> 5.42 us
  starting transfers between devices: 11.7 us -> 8 us
  Pallas kernels: 21.9 us -> 18.3 us
    all_to_all x2 -> x1, waiting for transfers between devices: 25.2 us -> 8.42 us  [exchange(): return lax.all_to_all(x, axis, 0, 0, tiled=True)]
    unnamed x39 -> x0, local copies, waits for them, and re-layouts: 8.63 us -> none
    all_to_all x3 -> x4, blocking collectives: 45.5 us -> 52.9 us  [exchange(): return lax.all_to_all(x, axis, 0, 0, tiled=True)]
    all_to_all x2 -> x1, starting transfers between devices: 11.7 us -> 8 us  [exchange(): return lax.all_to_all(x, axis, 0, 0, tiled=True)]
    pallas_call x1, Pallas kernels: 5.74 us -> 2.99 us  [step(): call(part(prompt_kernel, slots), [SMEM] + [VMEM] * 6, [((WIN, DK), BF16),...]
    pallas_call x1, Pallas kernels: 1.77 us -> 3.3 us  [step(): call(respond_kernel, [VMEM] * 5, [((2, RLEN, DV), F32), ((RLEN, LANES), F...]
    pallas_call x4, Pallas kernels: 10.3 us -> 8.76 us  [the longest x1 3.46 us: step(): call(part(state_kernel, slots), [HBM] * 5, [((SEQ, slots * STATE + AUX, L...]
    slice x0 -> x1, local copies, waits for them, and re-layouts: none -> 1.36 us  [local(): e2 = e1 + lengths[2]]
  transfers between devices with their start and end apart: 2 -> 1, of which waited for: 2 -> 1; matrix products, arithmetic and copies ran while one was open for 0% -> 0% of each run, Pallas kernels for 2% -> 3%
where the time goes in v2:
time: 95.4 us; the launch traced here: 94.9 us
  blocking collectives  52.9 us (55%)
  Pallas kernels  18.3 us (19%)
  waiting for transfers between devices  8.42 us (9%)
  starting transfers between devices  8 us (8%)
  between operations  5.42 us (6%)
  local copies, waits for them, and re-layouts  1.49 us (2%)
    all_to_all x4, blocking collectives, exchange(): return lax.all_to_all(x, axis, 0, 0, tiled=True)  52.9 us
    all_to_all x1, waiting for transfers between devices, exchange(): return lax.all_to_all(x, axis, 0, 0, tiled=True)  8.42 us
    all_to_all x1, starting transfers between devices, exchange(): return lax.all_to_all(x, axis, 0, 0, tiled=True)  8 us
    pallas_call x1, Pallas kernels, step(): call(part(state_kernel, slots), [HBM] * 5, [((SEQ, slots * STATE + AUX, L...  3.46 us
    pallas_call x1, Pallas kernels, step(): call(respond_kernel, [VMEM] * 5, [((2, RLEN, DV), F32), ((RLEN, LANES), F...  3.3 us
    pallas_call x1, Pallas kernels, step(): call(hidden_kernel, [SMEM] + [VMEM] * 6, [((2, RLEN, DV), F32), ((RLEN, L...  3.27 us
    pallas_call x1, Pallas kernels, step(): call(part(prompt_kernel, slots), [SMEM] + [VMEM] * 6, [((WIN, DK), BF16),...  2.99 us
    pallas_call x1, Pallas kernels, step(): call(grad_kernel, [VMEM] * 6, [((2, RLEN, DV), BF16), ((SEQ, 2 * STATE +...  2.74 us
  transfers between devices with their start and end apart: 1, of which 1 were waited for; matrix products, arithmetic and copies ran while one was open for 0% of the time, Pallas kernels for 3%

profile of v2, /device:TPU:0, one launch (start us, length us, event | category | flops | bytes accessed | tf_op | source)
XLA Modules:
  0.0 94.9 jit_solution(16905809861092953323)
XLA Ops:
  0.6 1.4 %fusion = (s32[1]{0:T(128)}, s32[1]{0:T(128)}, s32[1]{0:T(128)}) fusion(s32[4]{0:T(128)} %param.19), kind=kLoop, calls=%fused_computation | loop fusion | bytes 24 | tf_op jit(solution)/shard_map/slice | solution.py:514
  6.6 88.2 %conditional.1 = (bf16[2,512,512]{2,1,0:T(8,128)(2,1)}, bf16[1024,256]{1,0:T(8,128)(2,1)}, bf16[1024,512]{1,0:T(8,128)(2,1)}) conditional(s32[]{:T(128)} %convert_element_type.3, (s32[4]{0:T(128)}, bf16[1024,256]{1,0:T(8,128)(2,1)}, bf16[1024,512]{1,0:T(8,128)(2,1)}, f32[1,1024]{1,0:T(1,128)}, f32[1,1024]{1,0:T(1,128)}, ...), branch_computations={%region_0.1_spmd, %region_1.2_spmd} | conditional | bytes 20391028 | solution.py:517
  6.6 0.0 copy-start.16
  6.6 0.0 copy-start.12
  6.6 0.0 copy-start.14
  6.6 0.0 copy-start
  6.7 0.0 copy-start.8
  6.7 3.5 %state_kernel.2 = (bf16[16,136,128]{2,1,0:T(8,128)(2,1)}, f32[8,128]{1,0:T(8,128)S(1)}) custom-call(s32[4]{0:T(128)} %get-tuple-element.54.len_hbm.len_ref, bf16[1024,256]{1,0:T(8,128)(2,1)} %get-tuple-element.55.pk_hbm.pk, bf16[1024,512]{1,0:T(8,128)(2,1)} %get-tuple-element.56.pv_hbm.pv, f32[1,1024]{1,0:T(1,128)} %get-tuple-element.57.pin_hbm, ...), custom_call_target="tpu_custom_call" | custom-call | tf_op jit(solution)/shard_map/cond/branch_0_fun/state_kernel/pallas_call | solution.py:433
  10.1 8.0 %all-to-all-start = ((bf16[16,136,128]{2,1,0:T(8,128)(2,1)}), bf16[16,136,128]{2,1,0:T(8,128)(2,1)S(1)}, u32[]{:S(2)}, u32[]{:S(2)}) async-start(bf16[16,136,128]{2,1,0:T(8,128)(2,1)} %get-tuple-element.59), calls=%async_computation | async-start | bytes 1114112 | tf_op jit(solution)/shard_map/cond/branch_0_fun/all_to_all | solution.py:427
  18.1 0.0 copy-done.16
  18.2 0.1 copy.16.rp
  18.2 0.0 copy-done.12
  18.2 0.0 copy-done.14
  18.2 0.0 copy-start.10
  18.3 3.3 %respond_kernel.2 = (f32[2,512,512]{2,1,0:T(8,128)S(1)}, f32[512,128]{1,0:T(8,128)S(1)}) custom-call(bf16[2,512,256]{2,1,0:T(8,128)(2,1)} %get-tuple-element.53.q, bf16[2,512,256]{2,1,0:T(8,128)(2,1)} %get-tuple-element.61.k, bf16[2,512,512]{2,1,0:T(8,128)(2,1)} %get-tuple-element.62.v, f32[1,2,512]{2,1,0:T(2,128)S(1)} %copy-done.12, f32[1,2,512]{2,1,0:T(2,128)S(1)} %copy-done.14), custom_call_target="tpu_custom_call" | custom-call | tf_op jit(solution)/shard_map/cond/branch_0_fun/respond_kernel/pallas_call | solution.py:449
  21.6 8.4 %all-to-all-done.m = bf16[16,136,128]{2,1,0:T(8,128)(2,1)S(1)} async-done(((bf16[16,136,128]{2,1,0:T(8,128)(2,1)}), bf16[16,136,128]{2,1,0:T(8,128)(2,1)S(1)}, u32[]{:S(2)}, u32[]{:S(2)}) %all-to-all-start) | async-done | bytes 557088 | tf_op jit(solution)/shard_map/cond/branch_0_fun/all_to_all | solution.py:427
  30.0 0.0 copy-start.2
  30.0 0.0 copy-start.6
  30.0 0.0 copy-done
  30.0 0.0 copy-done.8
  30.0 1.5 %spread_kernel.2 = (bf16[16,144,128]{2,1,0:T(8,128)(2,1)S(1)}, f32[8,128]{1,0:T(8,128)S(1)}) custom-call(s32[4]{0:T(128)S(1)} %copy-done.8, s32[32,1]{1,0:T(8,128)S(1)} %copy.16.rp, bf16[16,136,128]{2,1,0:T(8,128)(2,1)S(1)} %all-to-all-done.m, f32[8,128]{1,0:T(8,128)S(1)} %get-tuple-element.60.expo, bf16[1024,256]{1,0:T(8,128)(2,1)S(1)} %copy-done, ...), custom_call_target="tpu_custom_call" | custom-call | tf_op jit(solution)/shard_map/cond/branch_0_fun/spread_kernel/pallas_call | solution.py:456
  31.5 14.4 %all_to_all.40.m = bf16[16,144,128]{2,1,0:T(8,128)(2,1)S(1)} all-to-all(bf16[16,144,128]{2,1,0:T(8,128)(2,1)S(1)} %get-tuple-element.66), channel_id=1, replica_groups=mesh['seq'=16,'head'=8] {'seq'}, dimensions={0} | all-to-all | bytes 1179648 | tf_op jit(solution)/shard_map/cond/branch_0_fun/all_to_all | solution.py:427
  45.9 0.0 copy-done.10
  45.9 0.0 copy-done.2
  45.9 0.0 copy-done.6
  45.9 3.3 %hidden_kernel.2 = (f32[2,512,512]{2,1,0:T(8,128)S(1)}, f32[512,128]{1,0:T(8,128)S(1)}, f32[8,16,128]{2,1,0:T(8,128)S(1)}) custom-call(s32[32,1]{1,0:T(8,128)S(1)} %copy.16.rp, bf16[2,512,256]{2,1,0:T(8,128)(2,1)S(1)} %copy-done.2, bf16[16,144,128]{2,1,0:T(8,128)(2,1)S(1)} %all_to_all.40.m, f32[2,512,512]{2,1,0:T(8,128)S(1)} %get-tuple-element.67.num, ...), custom_call_target="tpu_custom_call" | custom-call | tf_op jit(solution)/shard_map/cond/branch_0_fun/hidden_kernel/pallas_call | solution.py:468
  49.1 9.9 %all_to_all.41.m = f32[8,16,128]{2,1,0:T(8,128)S(1)} all-to-all(f32[8,16,128]{2,1,0:T(8,128)S(1)} %get-tuple-element.70), channel_id=1, replica_groups=mesh['seq'=16,'head'=8] {'head'}, dimensions={0} | all-to-all | bytes 131072 | tf_op jit(solution)/shard_map/cond/branch_0_fun/all_to_all | solution.py:427
  59.1 2.7 %grad_kernel.2 = (bf16[2,512,512]{2,1,0:T(8,128)(2,1)}, bf16[16,136,128]{2,1,0:T(8,128)(2,1)S(1)}) custom-call(f32[8,16,128]{2,1,0:T(8,128)S(1)} %all_to_all.41.m, f32[2,512,512]{2,1,0:T(8,128)S(1)} %get-tuple-element.71.hid, f32[512,128]{1,0:T(8,128)S(1)} %get-tuple-element.72.cols2, bf16[2,512,512]{2,1,0:T(8,128)(2,1)S(1)} %copy-done.6, ...), custom_call_target="tpu_custom_call" | custom-call | tf_op jit(solution)/shard_map/cond/branch_0_fun/grad_kernel/pallas_call | solution.py:476
  61.8 0.0 copy-start.4
  61.8 15.2 %all_to_all.42.m = bf16[16,136,128]{2,1,0:T(8,128)(2,1)S(1)} all-to-all(bf16[16,136,128]{2,1,0:T(8,128)(2,1)S(1)} %get-tuple-element.74), channel_id=1, replica_groups=mesh['seq'=16,'head'=8] {'seq'}, dimensions={0} | all-to-all | bytes 1114112 | tf_op jit(solution)/shard_map/cond/branch_0_fun/all_to_all | solution.py:427
  77.0 1.1 %gather_kernel.2 = (bf16[16,128,128]{2,1,0:T(8,128)(2,1)S(1)}, f32[8,256]{1,0:T(8,128)S(1)}) custom-call(s32[4]{0:T(128)S(1)} %copy-done.8, s32[32,1]{1,0:T(8,128)S(1)} %copy.16.rp, bf16[16,136,128]{2,1,0:T(8,128)(2,1)S(1)} %all_to_all.42.m), custom_call_target="tpu_custom_call" | custom-call | tf_op jit(solution)/shard_map/cond/branch_0_fun/gather_kernel/pallas_call | solution.py:484
  78.1 13.4 %all_to_all.43.m = bf16[16,128,128]{2,1,0:T(8,128)(2,1)S(1)} all-to-all(bf16[16,128,128]{2,1,0:T(8,128)(2,1)S(1)} %get-tuple-element.75), channel_id=1, replica_groups=mesh['seq'=16,'head'=8] {'seq'}, dimensions={0} | all-to-all | bytes 1048576 | tf_op jit(solution)/shard_map/cond/branch_0_fun/all_to_all | solution.py:427
  91.5 0.0 copy-done.4
  91.5 3.0 %prompt_kernel.2 = (bf16[1024,256]{1,0:T(8,128)(2,1)}, bf16[1024,512]{1,0:T(8,128)(2,1)}) custom-call(s32[4]{0:T(128)S(1)} %copy-done.8, bf16[16,128,128]{2,1,0:T(8,128)(2,1)S(1)} %all_to_all.43.m, f32[8,256]{1,0:T(8,128)S(1)} %get-tuple-element.76.gn, f32[8,128]{1,0:T(8,128)S(1)} %get-tuple-element.60.expo, f32[8,128]{1,0:T(8,128)S(1)} %get-tuple-element.77.aft, ...), custom_call_target="tpu_custom_call" | custom-call | tf_op jit(solution)/shard_map/cond/branch_0_fun/prompt_kernel/pallas_call | solution.py:496
Async XLA Ops:
  6.6 11.5 %copy-start.16 = (s32[32,1]{0,1:T(1,128)S(1)}, s32[32,1]{0,1:T(1,128)}, u32[]{:S(2)}) copy-start(s32[32,1]{0,1:T(1,128)} %get-tuple-element.121) | copy-start | bytes 388 | tf_op jit(solution)/shard_map/cond
  6.6 11.6 %copy-start.12 = (f32[1,2,512]{2,1,0:T(2,128)S(1)}, f32[1,2,512]{2,1,0:T(2,128)}, u32[]{:S(2)}) copy-start(f32[1,2,512]{2,1,0:T(2,128)} %get-tuple-element.63.rin) | copy-start | bytes 12292 | tf_op jit(solution)/shard_map/cond
  6.6 11.6 %copy-start.14 = (f32[1,2,512]{2,1,0:T(2,128)S(1)}, f32[1,2,512]{2,1,0:T(2,128)}, u32[]{:S(2)}) copy-start(f32[1,2,512]{2,1,0:T(2,128)} %get-tuple-element.64.rf) | copy-start | bytes 12292 | tf_op jit(solution)/shard_map/cond
  6.6 23.3 %copy-start = (bf16[1024,256]{1,0:T(8,128)(2,1)S(1)}, bf16[1024,256]{1,0:T(8,128)(2,1)}, u32[]{:S(2)}) copy-start(bf16[1024,256]{1,0:T(8,128)(2,1)} %get-tuple-element.55.pk_hbm.pk) | copy-start | bytes 1572868 | tf_op jit(solution)/shard_map/cond
  6.7 23.3 %copy-start.8 = (s32[4]{0:T(128)S(1)}, s32[4]{0:T(128)}, u32[]{:S(2)}) copy-start(s32[4]{0:T(128)} %get-tuple-element.54.len_hbm.len_ref) | copy-start | bytes 52 | tf_op jit(solution)/shard_map/cond
  10.1 19.8 %all-to-all-start = ((bf16[16,136,128]{2,1,0:T(8,128)(2,1)}), bf16[16,136,128]{2,1,0:T(8,128)(2,1)S(1)}, u32[]{:S(2)}, u32[]{:S(2)}) async-start(bf16[16,136,128]{2,1,0:T(8,128)(2,1)} %get-tuple-element.59), calls=%async_computation | async-start | bytes 1114112 | tf_op jit(solution)/shard_map/cond/branch_0_fun/all_to_all | solution.py:427
  18.2 27.6 %copy-start.10 = (f32[1,512]{1,0:T(1,128)S(1)}, f32[1,512]{1,0:T(1,128)}, u32[]{:S(2)}) copy-start(f32[1,512]{1,0:T(1,128)} %get-tuple-element.69.gain) | copy-start | bytes 6148 | tf_op jit(solution)/shard_map/cond
  30.0 15.9 %copy-start.2 = (bf16[2,512,256]{2,1,0:T(8,128)(2,1)S(1)}, bf16[2,512,256]{2,1,0:T(8,128)(2,1)}, u32[]{:S(2)}) copy-start(bf16[2,512,256]{2,1,0:T(8,128)(2,1)} %get-tuple-element.53.q) | copy-start | bytes 1572868 | tf_op jit(solution)/shard_map/cond
  30.0 15.9 %copy-start.6 = (bf16[2,512,512]{2,1,0:T(8,128)(2,1)S(1)}, bf16[2,512,512]{2,1,0:T(8,128)(2,1)}, u32[]{:S(2)}) copy-start(bf16[2,512,512]{2,1,0:T(8,128)(2,1)} %get-tuple-element.68.og) | copy-start | bytes 3145732 | tf_op jit(solution)/shard_map/cond
  61.8 29.7 %copy-start.4 = (bf16[1024,512]{1,0:T(8,128)(2,1)S(1)}, bf16[1024,512]{1,0:T(8,128)(2,1)}, u32[]{:S(2)}) copy-start(bf16[1024,512]{1,0:T(8,128)(2,1)} %get-tuple-element.56.pv_hbm.pv) | copy-start | bytes 3145732 | tf_op jit(solution)/shard_map/cond

commit v3 on v2

--- a/solution.py
+++ b/solution.py
@@ -35,7 +35,7 @@
     return pl.pallas_call(
         body,
         in_specs=ins,
-        out_specs=tuple(spec for _ in outs),
+        out_specs=spec if isinstance(spec, tuple) else tuple(spec for _ in outs),
         out_shape=tuple(jax.ShapeDtypeStruct(s, d) for s, d in outs),
         scratch_shapes=scratch,
         compiler_params=pltpu.CompilerParams(vmem_limit_bytes=24 << 20),
@@ -109,7 +109,7 @@
 
 
 def state_kernel(
-    slots, len_hbm, pk_hbm, pv_hbm, pin_hbm, pf_hbm, msg, e_out, len_ref, gates, inputs, pk, pv, wmat, sems
+    slots, len_hbm, pk_hbm, pv_hbm, pin_hbm, pf_hbm, msg, e_out, flag, len_ref, gates, inputs, pk, pv, wmat, sems
 ):
     me = lax.axis_index("seq")
     groups = WIN // LANES
@@ -125,6 +125,11 @@
     for copy in copies[:3]:
         copy.wait()
     ends = ends_of(len_ref)
+    crowded = jnp.int32(0)
+    for a, b in ((0, 1), (1, 2)):
+        inside = (ends[a] // WIN == ends[b] // WIN) & (ends[a] % WIN != 0)
+        crowded = jnp.where(inside, 1, crowded)
+    flag[0] = crowded
     shape = (groups, LANES)
     pid = window_pid(me, ends)
     lane, row = iota(shape, 1), iota(shape, 0)
@@ -265,7 +270,7 @@
             causal = iota((half, width), 0) + b * half >= iota((half, width), 1)
             decay = jnp.where(causal, ccol[rows, :] + srow[:, 0:width], -1e30)
             mixing = (scores * jnp.exp(decay)).astype(BF16)
-            num[r, rows, :] = dot(mixing, v[r, 0:width, :], 1, 0)
+            num[r, rows, :] = dot(mixing, v[r, 0:width, :], 1, 0).astype(BF16)
             den = jnp.sum(mixing.astype(F32), axis=1, keepdims=True)
             cols[rows, :] = jnp.where(
                 clane[rows, :] == r, den, packed[rows, :] if r == 0 else cols[rows, :]
@@ -279,33 +284,43 @@
     aux = jnp.sum(m[:, 2 * STATE : 2 * STATE + NAUX, :].astype(F32), axis=0)
     aux = aux[0:8, :] + aux[8:16, :]
     nrm[0:PROMPTS, :] = jnp.concatenate([aux[0:PROMPTS, :], aux[PROMPTS:8, :]], axis=1)
-    clane = iota((RLEN, LANES), 1)
-    sums = jnp.zeros((RLEN, LANES), F32)
-    packed = jnp.zeros((RLEN, LANES), F32)
+    clane = iota((GROUP, LANES), 1)
+    sums = [jnp.zeros((GROUP, LANES), F32) for _ in range(RLEN // GROUP)]
     for r in range(2):
         norm = jnp.broadcast_to(nrm[pl.ds(rp[2 * me + r, 0], 1), :], (LANES, DK)).astype(BF16)
-        lifted = cols[:, 2 + r : 3 + r]
-        qn = dot(q[r], norm, 1, 1)[:, 0:1]
-        den = cols[:, r : r + 1] + lifted * qn
-        inverse = lax.rsqrt(den * den + 1.0)
-        hidden = (num[r] + lifted * dot(q[r], received(m, r), 1, 0)) * inverse
-        hid[r] = hidden
-        squares = jnp.sum(hidden * hidden, axis=1, keepdims=True)
-        dots = jnp.sum(og[r].astype(F32) * gain[...] * hidden, axis=1, keepdims=True)
-        sums = jnp.where(clane == 2 * r, squares, jnp.where(clane == 2 * r + 1, dots, sums))
-        lift = lifted * inverse
-        ratio = lifted * den * (inverse * inverse)
-        packed = jnp.where(clane == 4 + r, lift, jnp.where(clane == 6 + r, ratio, packed))
-    cols2[...] = packed + sums
-    rows = sums.T
-    rows = jnp.concatenate(
-        [rows[0:4, c * LANES : (c + 1) * LANES] for c in range(RLEN // LANES)], axis=0
-    )
+        state = received(m, r)
+        for b in range(RLEN // GROUP):
+            rows = slice(b * GROUP, (b + 1) * GROUP)
+            small = cols[rows, :]
+            lifted = small[:, 2 + r : 3 + r]
+            query = q[r, rows, :]
+            den = small[:, r : r + 1] + lifted * dot(query, norm, 1, 1)[:, 0:1]
+            inverse = lax.rsqrt(den * den + 1.0)
+            hidden = (num[r, rows, :].astype(F32) + lifted * dot(query, state, 1, 0)) * inverse
+            hid[r, rows, :] = hidden.astype(BF16)
+            squares = jnp.sum(hidden * hidden, axis=1, keepdims=True)
+            dots = jnp.sum(og[r, rows, :].astype(F32) * gain[...] * hidden, axis=1, keepdims=True)
+            lift = lifted * inverse
+            total = sums[b]
+            for at, value in (
+                (2 * r, squares),
+                (2 * r + 1, dots),
+                (4 + r, lift),
+                (6 + r, den * inverse * lift),
+            ):
+                total = jnp.where(clane == at, value, total)
+            sums[b] = total
+    rows8 = []
+    for b in range(RLEN // GROUP):
+        cols2[b * GROUP : (b + 1) * GROUP, :] = sums[b]
+        turned = sums[b].T
+        rows8 += [turned[0:4, c * LANES : (c + 1) * LANES] for c in range(GROUP // LANES)]
+    rows = jnp.concatenate(rows8, axis=0)
     for dev in range(HEADS):
         msg[dev] = rows
 
 
-def grad_kernel(m, hid, cols2, og, gain, q, out, msg, numer, denom):
+def grad_kernel(m, hid, cols2, og, gain, q, msg, inv_out, numer, denom):
     total = m[0]
     for dev in range(1, HEADS):
         total = total + m[dev]
@@ -313,6 +328,7 @@
     total = jnp.concatenate([total, jnp.zeros((LANES - 16, LANES), F32)], axis=0).T
     inverses = lax.rsqrt(total / features + 1e-6)
     coefs = pltpu.roll(total, LANES - 1, 1) * (inverses * inverses * inverses) / features
+    inv_out[...] = inverses
     rows8 = []
     for r in range(2):
         for c in range(RLEN // LANES):
@@ -321,12 +337,10 @@
             inv, coef = inverses[:, at : at + 1], coefs[:, at : at + 1]
             small = cols2[rows, :]
             squares, dots = small[:, 2 * r : 2 * r + 1], small[:, 2 * r + 1 : 2 * r + 2]
-            lift, ratio = small[:, 4 + r : 5 + r], small[:, 6 + r : 7 + r]
-            hidden = hid[r, rows, :]
-            scaled = gain[...] * inv
-            out[r, rows, :] = (hidden * scaled).astype(BF16)
-            d_hidden = scaled * og[r, rows, :].astype(F32) - hidden * coef
-            numer[rows, :] = (lift * d_hidden).astype(BF16)
+            ratio = small[:, 6 + r : 7 + r]
+            lift = small[:, 4 + r : 5 + r]
+            grads = gain[...] * og[r, rows, :].astype(F32)
+            numer[rows, :] = (grads * (inv * lift) - hid[r, rows, :].astype(F32) * (coef * lift)).astype(BF16)
             lift_denom = (-(inv * dots - coef * squares) * ratio).astype(BF16).astype(F32)
             part = jnp.sum(lift_denom * q[r, rows, :].astype(F32), axis=0, keepdims=True)
             denom[...] = part if c == 0 else denom[...] + part
@@ -341,7 +355,30 @@
         msg[dev, 2 * STATE : 2 * STATE + AUX, :] = aux
 
 
-def gather_kernel(slots, len_ref, rp, m, out, gn, acc, aacc, low):
+def out_kernel(len_ref, hid, inverses, gain, expo, aft, pk, out, columns_out, weighted):
+    me = lax.axis_index("seq")
+    groups = WIN // LANES
+    pid = window_pid(me, ends_of(len_ref))
+    after = jnp.zeros((groups, LANES), F32)
+    for p in range(PROMPTS):
+        after = jnp.where(pid == p, aft[0:1, p : p + 1], after)
+    weight = jnp.exp(expo[...] + after)
+    columns = jnp.concatenate(
+        [weight, pid.astype(F32), jnp.zeros((LANES - 2 * groups, LANES), F32)], axis=0
+    ).T
+    columns_out[...] = columns
+    for r in range(groups):
+        rows = slice(r * LANES, (r + 1) * LANES)
+        weighted[rows, :] = (pk[rows, :].astype(F32) * columns[:, r : r + 1]).astype(BF16)
+    for r in range(2):
+        for c in range(RLEN // LANES):
+            rows = slice(c * LANES, (c + 1) * LANES)
+            at = 4 * c + 2 * r
+            inv = inverses[:, at : at + 1]
+            out[r, rows, :] = (hid[r, rows, :].astype(F32) * gain[...] * inv).astype(BF16)
+
+
+def gather_kernel(slots, len_ref, rp, m, unused, out, gn, acc, aacc, low):
     ends = ends_of(len_ref)
     acc[...] = jnp.zeros_like(acc)
     aacc[...] = jnp.zeros_like(aacc)
@@ -364,20 +401,14 @@
             out[dev, s * STATE : (s + 1) * STATE, :] = low[jnp.minimum(first + s, PROMPTS - 1)]
 
 
-def prompt_kernel(slots, len_ref, m, gn, expo, aft, pk, pv, kg_hbm, vg_hbm, kg, vg, sems):
+def prompt_kernel(
+    slots, len_ref, m, gn, columns_ref, weighted_ref, pv, kg_hbm, vg_hbm, kg, vg, sems
+):
     me = lax.axis_index("seq")
     ends = ends_of(len_ref)
     groups = WIN // LANES
-    pid = window_pid(me, ends)
-    after = jnp.zeros((groups, LANES), F32)
-    for p in range(PROMPTS):
-        after = jnp.where(pid == p, aft[0:1, p : p + 1], after)
-    weight = jnp.exp(expo[...] + after)
     first = first_prompt(me, ends, slots)
-    stacked = jnp.concatenate(
-        [weight, pid.astype(F32), jnp.zeros((LANES - 2 * groups, LANES), F32)], axis=0
-    )
-    columns = stacked.T
+    columns = columns_ref[...]
 
     def at_row(j):
         total = jnp.int32(0)
@@ -395,7 +426,7 @@
             )
             for at in (0, groups)
         )
-        weighted = (pk[rows, :].astype(F32) * w).astype(BF16)
+        weighted = weighted_ref[rows, :]
         low, high = at_row(g * GROUP), at_row((g + 1) * GROUP - 1)
 
         def grads(p):
@@ -427,13 +458,16 @@
     return lax.all_to_all(x, axis, 0, 0, tiled=True)
 
 
-def step(slots, pk, pv, pin, pf, lengths, rp, q, k, v, rin, rf, gain, og):
+def states(slots, pk, pv, pin, pf, lengths):
     groups = WIN // LANES
-    part = functools.partial
-    msg1, expo = call(
-        part(state_kernel, slots),
+    return call(
+        functools.partial(state_kernel, slots),
         [HBM] * 5,
-        [((SEQ, slots * STATE + AUX, LANES), BF16), ((groups, LANES), F32)],
+        [
+            ((SEQ, slots * STATE + AUX, LANES), BF16),
+            ((groups, LANES), F32),
+            ((1,), jnp.int32),
+        ],
         [
             pltpu.SMEM((PROMPTS,), jnp.int32),
             pltpu.VMEM((1, WIN), F32),
@@ -443,16 +477,16 @@
             pltpu.VMEM((slots, WIN, DK), BF16),
             pltpu.SemaphoreType.DMA((5,)),
         ],
+        spec=(VMEM, VMEM, SMEM),
         name="state_kernel",
     )(lengths, pk, pv, pin, pf)
-    got1 = exchange(msg1, "seq")
-    num, cols = call(
-        respond_kernel,
-        [VMEM] * 5,
-        [((2, RLEN, DV), F32), ((RLEN, LANES), F32)],
-        [],
-        name="respond_kernel",
-    )(q, k, v, rin, rf)
+
+
+def rest(slots, got1, expo, num, cols, pk, pv, pin, pf, lengths, rp, q, gain, og):
+    part = functools.partial
+    if slots > 2:
+        msg1, expo, _ = states(slots, pk, pv, pin, pf, lengths)
+        got1 = exchange(msg1, "seq")
     msg2, aft = call(
         part(spread_kernel, slots),
         [SMEM, SMEM] + [VMEM] * 3 + [ANY],
@@ -468,22 +502,29 @@
     hid, cols2, msg3 = call(
         hidden_kernel,
         [SMEM] + [VMEM] * 6,
-        [((2, RLEN, DV), F32), ((RLEN, LANES), F32), ((HEADS, 16, LANES), F32)],
+        [((2, RLEN, DV), BF16), ((RLEN, LANES), F32), ((HEADS, 16, LANES), F32)],
         [pltpu.VMEM((8, DK), F32)],
         name="hidden_kernel",
     )(rp, q, got2, num, cols, og, gain)
     got3 = exchange(msg3, "head")
-    resp_out, msg4 = call(
+    msg4, inverses = call(
         grad_kernel,
         [VMEM] * 6,
-        [((2, RLEN, DV), BF16), ((SEQ, 2 * STATE + AUX, LANES), BF16)],
+        [((SEQ, 2 * STATE + AUX, LANES), BF16), ((LANES, LANES), F32)],
         [pltpu.VMEM((RLEN, DV), BF16), pltpu.VMEM((1, DK), F32)],
         name="grad_kernel",
     )(got3, hid, cols2, og, gain, q)
     got4 = exchange(msg4, "seq")
+    resp_out, columns, weighted = call(
+        out_kernel,
+        [SMEM] + [VMEM] * 6,
+        [((2, RLEN, DV), BF16), ((LANES, LANES), F32), ((WIN, DK), BF16)],
+        [],
+        name="out_kernel",
+    )(lengths, hid, inverses, gain, expo, aft, pk)
     msg5, gn = call(
         part(gather_kernel, slots),
-        [SMEM, SMEM, VMEM],
+        [SMEM, SMEM, VMEM, ANY],
         [((SEQ, slots * STATE, LANES), BF16), ((8, DK), F32)],
         [
             pltpu.VMEM((PROMPTS, STATE, LANES), F32),
@@ -491,11 +532,11 @@
             pltpu.VMEM((PROMPTS, STATE, LANES), BF16),
         ],
         name="gather_kernel",
-    )(lengths, rp, got4)
+    )(lengths, rp, got4, columns)
     got5 = exchange(msg5, "seq")
     key_grad, value_grad = call(
         part(prompt_kernel, slots),
-        [SMEM] + [VMEM] * 6,
+        [SMEM] + [VMEM] * 5,
         [((WIN, DK), BF16), ((WIN, DV), BF16)],
         [
             pltpu.VMEM((WIN, DK), BF16),
@@ -504,18 +545,23 @@
         ],
         spec=HBM,
         name="prompt_kernel",
-    )(lengths, got5, gn, expo, aft, pk, pv)
+    )(lengths, got5, gn, columns, weighted, pv)
     return resp_out, key_grad, value_grad
 
 
 def local(pk, pv, pin, pf, lengths, rp, q, k, v, rin, rf, gain, og):
-    e0 = lengths[0]
-    e1 = e0 + lengths[1]
-    e2 = e1 + lengths[2]
-    crowded = ((e0 // WIN == e1 // WIN) & (e0 % WIN != 0)) | ((e1 // WIN == e2 // WIN) & (e1 % WIN != 0))
-    args = (pk, pv, pin, pf, lengths, rp, q, k, v, rin, rf, gain.reshape(1, DV), og)
+    msg1, expo, flag = states(2, pk, pv, pin, pf, lengths)
+    got1 = exchange(msg1, "seq")
+    num, cols = call(
+        respond_kernel,
+        [VMEM] * 5,
+        [((2, RLEN, DV), BF16), ((RLEN, LANES), F32)],
+        [],
+        name="respond_kernel",
+    )(q, k, v, rin, rf)
+    args = (got1, expo, num, cols, pk, pv, pin, pf, lengths, rp, q, gain.reshape(1, DV), og)
     return lax.cond(
-        crowded, functools.partial(step, PROMPTS), functools.partial(step, 2), *args
+        flag[0] > 0, functools.partial(rest, PROMPTS), functools.partial(rest, 2), *args
     )
 
 

time: 95.4 us -> 90.9 us (0.953)
  blocking collectives: 52.9 us -> 38.1 us
  waiting for transfers between devices: 8.42 us -> 17.1 us
  between operations: 5.42 us -> 1.74 us
  starting transfers between devices: 8 us -> 11.6 us
  Pallas kernels: 18.3 us -> 21.5 us
  local copies, waits for them, and re-layouts: 1.49 us -> 0.16 us
    all_to_all x4 -> x3, blocking collectives: 52.9 us -> 38.1 us  [exchange(): return lax.all_to_all(x, axis, 0, 0, tiled=True)]
    all_to_all x1 -> x2, waiting for transfers between devices: 8.42 us -> 17.1 us  [exchange(): return lax.all_to_all(x, axis, 0, 0, tiled=True)]
    all_to_all x1 -> x2, starting transfers between devices: 8 us -> 11.6 us  [exchange(): return lax.all_to_all(x, axis, 0, 0, tiled=True)]
    pallas_call x7 -> x8, Pallas kernels: 18.3 us -> 21.5 us  [the longest x1 3.81 us: local(): call(respond_kernel, [VMEM] * 5, [((2, RLEN, DV), BF16), ((RLEN, LANES),...]
    slice x1 -> x0, local copies, waits for them, and re-layouts: 1.36 us -> none  [local(): e2 = e1 + lengths[2]]
  transfers between devices with their start and end apart: 1 -> 2, of which waited for: 1 -> 2; matrix products, arithmetic and copies ran while one was open for 0% -> 0% of each run, Pallas kernels for 3% -> 7%
where the time goes in v3:
time: 90.9 us; the launch traced here: 90.4 us
  blocking collectives  38.1 us (42%)
  Pallas kernels  21.5 us (24%)
  waiting for transfers between devices  17.1 us (19%)
  starting transfers between devices  11.6 us (13%)
  between operations  1.74 us (2%)
    all_to_all x3, blocking collectives, exchange(): return lax.all_to_all(x, axis, 0, 0, tiled=True)  38.1 us
    all_to_all x2, waiting for transfers between devices, exchange(): return lax.all_to_all(x, axis, 0, 0, tiled=True)  17.1 us
    all_to_all x2, starting transfers between devices, exchange(): return lax.all_to_all(x, axis, 0, 0, tiled=True)  11.6 us
    pallas_call x1, Pallas kernels, local(): call(respond_kernel, [VMEM] * 5, [((2, RLEN, DV), BF16), ((RLEN, LANES),...  3.81 us
    pallas_call x1, Pallas kernels, rest(): call(hidden_kernel, [SMEM] + [VMEM] * 6, [((2, RLEN, DV), BF16), ((RLEN,...  3.51 us
    pallas_call x1, Pallas kernels, states(): call(functools.partial(state_kernel, slots), [HBM] * 5, [((SEQ, slots * S...  3.49 us
    pallas_call x1, Pallas kernels, rest(): call(grad_kernel, [VMEM] * 6, [((SEQ, 2 * STATE + AUX, LANES), BF16), ((L...  2.98 us
    pallas_call x1, Pallas kernels, rest(): call(part(prompt_kernel, slots), [SMEM] + [VMEM] * 5, [((WIN, DK), BF16),...  2.61 us
  transfers between devices with their start and end apart: 2, of which 2 were waited for; matrix products, arithmetic and copies ran while one was open for 0% of the time, Pallas kernels for 7%

profile of v3, /device:TPU:0, one launch (start us, length us, event | category | flops | bytes accessed | tf_op | source)
XLA Modules:
  0.0 90.4 jit_solution(2141097875500182776)
XLA Ops:
  0.6 0.0 copy-start.3
  0.6 0.0 copy-start.2
  0.7 0.0 copy-start
  0.7 0.0 copy-start.1
  0.7 3.5 %state_kernel.3 = (bf16[16,136,128]{2,1,0:T(8,128)(2,1)}, f32[8,128]{1,0:T(8,128)S(1)}, s32[1]{0:T(128)}) custom-call(s32[4]{0:T(128)} %len_hbm.1, bf16[1024,256]{1,0:T(8,128)(2,1)} %pk_hbm.1, bf16[1024,512]{1,0:T(8,128)(2,1)} %pv_hbm.1, f32[1,1024]{1,0:T(1,128)} %pin_hbm.1, f32[1,1024]{1,0:T(1,128)} %pf_hbm.1), custom_call_target="tpu_custom_call" | custom-call | tf_op jit(solution)/shard_map/state_kernel/pallas_call | solution.py:463
  4.2 8.0 %all-to-all-start.9 = ((bf16[16,136,128]{2,1,0:T(8,128)(2,1)}), bf16[16,136,128]{2,1,0:T(8,128)(2,1)}, u32[]{:S(2)}, u32[]{:S(2)}) async-start(bf16[16,136,128]{2,1,0:T(8,128)(2,1)} %get-tuple-element.105), calls=%async_computation.9 | async-start | bytes 1114112 | tf_op jit(solution)/shard_map/all_to_all | solution.py:458
  12.2 0.0 copy-start.4
  12.2 0.0 copy-start.5
  12.2 0.0 copy-start.13
  12.3 0.0 copy-start.14
  12.3 0.0 copy-start.15
  12.3 0.0 copy-start.16
  12.3 0.0 copy-start.17
  13.1 0.0 copy-done.3
  13.1 0.0 copy-done.2
  13.1 0.0 copy-done
  13.1 0.0 copy-done.1
  13.1 3.8 %respond_kernel.1 = (bf16[2,512,512]{2,1,0:T(8,128)(2,1)}, f32[512,128]{1,0:T(8,128)S(1)}) custom-call(bf16[2,512,256]{2,1,0:T(8,128)(2,1)} %q.1, bf16[2,512,256]{2,1,0:T(8,128)(2,1)S(1)} %copy-done.1, bf16[2,512,512]{2,1,0:T(8,128)(2,1)S(1)} %copy-done, f32[1,2,512]{2,1,0:T(2,128)S(1)} %copy-done.2, f32[1,2,512]{2,1,0:T(2,128)S(1)} %copy-done.3), custom_call_target="tpu_custom_call" | custom-call | tf_op jit(solution)/shard_map/respond_kernel/pallas_call | solution.py:555
  16.9 7.2 %all-to-all-done.9 = bf16[16,136,128]{2,1,0:T(8,128)(2,1)} async-done(((bf16[16,136,128]{2,1,0:T(8,128)(2,1)}), bf16[16,136,128]{2,1,0:T(8,128)(2,1)}, u32[]{:S(2)}, u32[]{:S(2)}) %all-to-all-start.9) | async-done | bytes 557088 | tf_op jit(solution)/shard_map/all_to_all | solution.py:458
  24.1 0.0 copy-done.4
  24.1 0.0 copy-done.5
  24.1 0.0 copy-done.13
  24.1 0.0 copy-done.14
  24.1 0.0 copy-done.15
  24.2 0.0 copy-done.16
  24.2 0.0 copy-done.17
  24.2 66.0 %conditional.1 = (bf16[2,512,512]{2,1,0:T(8,128)(2,1)}, bf16[1024,256]{1,0:T(8,128)(2,1)}, bf16[1024,512]{1,0:T(8,128)(2,1)}) conditional(s32[]{:T(128)} %bitcast, (s32[4]{0:T(128)S(1)}, s32[32,1]{0,1:T(1,128)S(1)}, bf16[16,136,128]{2,1,0:T(8,128)(2,1)}, f32[8,128]{1,0:T(8,128)S(1)}, bf16[1024,256]{1,0:T(8,128)(2,1)S(1)}, ...), branch_computations={%region_0.0_spmd, %region_1.0_spmd} | conditional | bytes 23003592 | solution.py:563
  24.2 0.1 copy.16.rp
  24.3 0.0 copy-start.9
  24.3 0.0 copy-start.11
  24.3 1.9 %spread_kernel.2 = (bf16[16,144,128]{2,1,0:T(8,128)(2,1)S(1)}, f32[8,128]{1,0:T(8,128)S(1)}) custom-call(s32[4]{0:T(128)S(1)} %get-tuple-element.44.len_ref, s32[32,1]{1,0:T(8,128)S(1)} %copy.16.rp, bf16[16,136,128]{2,1,0:T(8,128)(2,1)} %get-tuple-element.47.m, f32[8,128]{1,0:T(8,128)S(1)} %get-tuple-element.48.expo, ...), custom_call_target="tpu_custom_call" | custom-call | tf_op jit(solution)/shard_map/cond/branch_0_fun/spread_kernel/pallas_call | solution.py:490
  26.2 14.4 %all_to_all.41.m = bf16[16,144,128]{2,1,0:T(8,128)(2,1)S(1)} all-to-all(bf16[16,144,128]{2,1,0:T(8,128)(2,1)S(1)} %get-tuple-element.51), channel_id=1, replica_groups=mesh['seq'=16,'head'=8] {'seq'}, dimensions={0} | all-to-all | bytes 1179648 | tf_op jit(solution)/shard_map/cond/branch_0_fun/all_to_all | solution.py:458
  40.5 0.0 copy-done.9
  40.5 0.0 copy-done.11
  40.5 3.5 %hidden_kernel.2 = (bf16[2,512,512]{2,1,0:T(8,128)(2,1)S(1)}, f32[512,128]{1,0:T(8,128)S(1)}, f32[8,16,128]{2,1,0:T(8,128)S(1)}) custom-call(s32[32,1]{1,0:T(8,128)S(1)} %copy.16.rp, bf16[2,512,256]{2,1,0:T(8,128)(2,1)S(1)} %copy-done.9, bf16[16,144,128]{2,1,0:T(8,128)(2,1)S(1)} %all_to_all.41.m, bf16[2,512,512]{2,1,0:T(8,128)(2,1)S(1)} %copy-done.11, ...), custom_call_target="tpu_custom_call" | custom-call | tf_op jit(solution)/shard_map/cond/branch_0_fun/hidden_kernel/pallas_call | solution.py:502
  44.1 9.9 %all_to_all.42.m = f32[8,16,128]{2,1,0:T(8,128)S(1)} all-to-all(f32[8,16,128]{2,1,0:T(8,128)S(1)} %get-tuple-element.56), channel_id=1, replica_groups=mesh['seq'=16,'head'=8] {'head'}, dimensions={0} | all-to-all | bytes 131072 | tf_op jit(solution)/shard_map/cond/branch_0_fun/all_to_all | solution.py:458
  54.0 3.0 %grad_kernel.2 = (bf16[16,136,128]{2,1,0:T(8,128)(2,1)}, f32[128,128]{1,0:T(8,128)S(1)}) custom-call(f32[8,16,128]{2,1,0:T(8,128)S(1)} %all_to_all.42.m, bf16[2,512,512]{2,1,0:T(8,128)(2,1)S(1)} %get-tuple-element.55.hid, f32[512,128]{1,0:T(8,128)S(1)} %get-tuple-element.57.cols2, bf16[2,512,512]{2,1,0:T(8,128)(2,1)S(1)} %get-tuple-element.53.og, ...), custom_call_target="tpu_custom_call" | custom-call | tf_op jit(solution)/shard_map/cond/branch_0_fun/grad_kernel/pallas_call | solution.py:510
  56.9 3.6 %all-to-all-start.2 = ((bf16[16,136,128]{2,1,0:T(8,128)(2,1)}), bf16[16,136,128]{2,1,0:T(8,128)(2,1)S(1)}, u32[]{:S(2)}, u32[]{:S(2)}) async-start(bf16[16,136,128]{2,1,0:T(8,128)(2,1)} %get-tuple-element.61), calls=%async_computation.2 | async-start | bytes 1114112 | tf_op jit(solution)/shard_map/cond/branch_0_fun/all_to_all | solution.py:458
  60.5 2.1 %out_kernel.2 = (bf16[2,512,512]{2,1,0:T(8,128)(2,1)}, f32[128,128]{1,0:T(8,128)S(1)}, bf16[1024,256]{1,0:T(8,128)(2,1)S(1)}) custom-call(s32[4]{0:T(128)S(1)} %get-tuple-element.44.len_ref, bf16[2,512,512]{2,1,0:T(8,128)(2,1)S(1)} %get-tuple-element.55.hid, f32[128,128]{1,0:T(8,128)S(1)} %get-tuple-element.58.inverses, ...), custom_call_target="tpu_custom_call" | custom-call | tf_op jit(solution)/shard_map/cond/branch_0_fun/out_kernel/pallas_call | solution.py:518
  62.7 9.8 %all-to-all-done.2.m = bf16[16,136,128]{2,1,0:T(8,128)(2,1)S(1)} async-done(((bf16[16,136,128]{2,1,0:T(8,128)(2,1)}), bf16[16,136,128]{2,1,0:T(8,128)(2,1)S(1)}, u32[]{:S(2)}, u32[]{:S(2)}) %all-to-all-start.2) | async-done | bytes 557088 | tf_op jit(solution)/shard_map/cond/branch_0_fun/all_to_all | solution.py:458
  72.5 0.0 copy-start.7
  72.5 1.1 %gather_kernel.2 = (bf16[16,128,128]{2,1,0:T(8,128)(2,1)S(1)}, f32[8,256]{1,0:T(8,128)S(1)}) custom-call(s32[4]{0:T(128)S(1)} %get-tuple-element.44.len_ref, s32[32,1]{1,0:T(8,128)S(1)} %copy.16.rp, bf16[16,136,128]{2,1,0:T(8,128)(2,1)S(1)} %all-to-all-done.2.m, f32[128,128]{1,0:T(8,128)S(1)} %get-tuple-element.62.unused.columns_ref), custom_call_target="tpu_custom_call" | custom-call | tf_op jit(solution)/shard_map/cond/branch_0_fun/gather_kernel/pallas_call | solution.py:525
  73.6 13.8 %all_to_all.43.m = bf16[16,128,128]{2,1,0:T(8,128)(2,1)S(1)} all-to-all(bf16[16,128,128]{2,1,0:T(8,128)(2,1)S(1)} %get-tuple-element.63), channel_id=1, replica_groups=mesh['seq'=16,'head'=8] {'seq'}, dimensions={0} | all-to-all | bytes 1048576 | tf_op jit(solution)/shard_map/cond/branch_0_fun/all_to_all | solution.py:458
  87.4 0.0 copy-done.7
  87.4 2.6 %prompt_kernel.2 = (bf16[1024,256]{1,0:T(8,128)(2,1)}, bf16[1024,512]{1,0:T(8,128)(2,1)}) custom-call(s32[4]{0:T(128)S(1)} %get-tuple-element.44.len_ref, bf16[16,128,128]{2,1,0:T(8,128)(2,1)S(1)} %all_to_all.43.m, f32[8,256]{1,0:T(8,128)S(1)} %get-tuple-element.64.gn, f32[128,128]{1,0:T(8,128)S(1)} %get-tuple-element.62.unused.columns_ref, ...), custom_call_target="tpu_custom_call" | custom-call | tf_op jit(solution)/shard_map/cond/branch_0_fun/prompt_kernel/pallas_call | solution.py:537
Async XLA Ops:
  0.6 12.4 %copy-start.3 = (f32[1,2,512]{2,1,0:T(2,128)S(1)}, f32[1,2,512]{2,1,0:T(2,128)}, u32[]{:S(2)}) copy-start(f32[1,2,512]{2,1,0:T(2,128)} %rf.1) | copy-start | bytes 12292
  0.6 12.4 %copy-start.2 = (f32[1,2,512]{2,1,0:T(2,128)S(1)}, f32[1,2,512]{2,1,0:T(2,128)}, u32[]{:S(2)}) copy-start(f32[1,2,512]{2,1,0:T(2,128)} %rin.1) | copy-start | bytes 12292
  0.7 12.4 %copy-start = (bf16[2,512,512]{2,1,0:T(8,128)(2,1)S(1)}, bf16[2,512,512]{2,1,0:T(8,128)(2,1)}, u32[]{:S(2)}) copy-start(bf16[2,512,512]{2,1,0:T(8,128)(2,1)} %v.1) | copy-start | bytes 3145732
  0.7 12.4 %copy-start.1 = (bf16[2,512,256]{2,1,0:T(8,128)(2,1)S(1)}, bf16[2,512,256]{2,1,0:T(8,128)(2,1)}, u32[]{:S(2)}) copy-start(bf16[2,512,256]{2,1,0:T(8,128)(2,1)} %k.1) | copy-start | bytes 1572868
  4.2 20.0 %all-to-all-start.9 = ((bf16[16,136,128]{2,1,0:T(8,128)(2,1)}), bf16[16,136,128]{2,1,0:T(8,128)(2,1)}, u32[]{:S(2)}, u32[]{:S(2)}) async-start(bf16[16,136,128]{2,1,0:T(8,128)(2,1)} %get-tuple-element.105), calls=%async_computation.9 | async-start | bytes 1114112 | tf_op jit(solution)/shard_map/all_to_all | solution.py:458
  12.2 11.9 %copy-start.4 = (bf16[1024,256]{1,0:T(8,128)(2,1)S(1)}, bf16[1024,256]{1,0:T(8,128)(2,1)}, u32[]{:S(2)}) copy-start(bf16[1024,256]{1,0:T(8,128)(2,1)} %pk_hbm.1) | copy-start | bytes 1572868
  12.2 11.9 %copy-start.5 = (bf16[2,512,512]{2,1,0:T(8,128)(2,1)S(1)}, bf16[2,512,512]{2,1,0:T(8,128)(2,1)}, u32[]{:S(2)}) copy-start(bf16[2,512,512]{2,1,0:T(8,128)(2,1)} %param.27) | copy-start | bytes 3145732
  12.2 11.9 %copy-start.13 = (f32[512]{0:T(512)S(1)}, f32[512]{0:T(512)}, u32[]{:S(2)}) copy-start(f32[512]{0:T(512)} %param.26) | copy-start | bytes 6148
  12.3 11.9 %copy-start.14 = (s32[4]{0:T(128)S(1)}, s32[4]{0:T(128)}, u32[]{:S(2)}) copy-start(s32[4]{0:T(128)} %len_hbm.1) | copy-start | bytes 52
  12.3 11.9 %copy-start.15 = (f32[1,1024]{1,0:T(1,128)S(1)}, f32[1,1024]{1,0:T(1,128)}, u32[]{:S(2)}) copy-start(f32[1,1024]{1,0:T(1,128)} %pin_hbm.1) | copy-start | bytes 12292
  12.3 11.9 %copy-start.16 = (f32[1,1024]{1,0:T(1,128)S(1)}, f32[1,1024]{1,0:T(1,128)}, u32[]{:S(2)}) copy-start(f32[1,1024]{1,0:T(1,128)} %pf_hbm.1) | copy-start | bytes 12292
  12.3 11.9 %copy-start.17 = (s32[32,1]{0,1:T(1,128)S(1)}, s32[32,1]{0,1:T(1,128)}, u32[]{:S(2)}) copy-start(s32[32,1]{0,1:T(1,128)} %param.20) | copy-start | bytes 388
  24.3 16.3 %copy-start.9 = (bf16[2,512,256]{2,1,0:T(8,128)(2,1)S(1)}, bf16[2,512,256]{2,1,0:T(8,128)(2,1)}, u32[]{:S(2)}) copy-start(bf16[2,512,256]{2,1,0:T(8,128)(2,1)} %get-tuple-element.46.q) | copy-start | bytes 1572868 | tf_op jit(solution)/shard_map/cond
  24.3 16.3 %copy-start.11 = (bf16[2,512,512]{2,1,0:T(8,128)(2,1)S(1)}, bf16[2,512,512]{2,1,0:T(8,128)(2,1)}, u32[]{:S(2)}) copy-start(bf16[2,512,512]{2,1,0:T(8,128)(2,1)} %get-tuple-element.52.num) | copy-start | bytes 3145732 | tf_op jit(solution)/shard_map/cond
  56.9 15.6 %all-to-all-start.2 = ((bf16[16,136,128]{2,1,0:T(8,128)(2,1)}), bf16[16,136,128]{2,1,0:T(8,128)(2,1)S(1)}, u32[]{:S(2)}, u32[]{:S(2)}) async-start(bf16[16,136,128]{2,1,0:T(8,128)(2,1)} %get-tuple-element.61), calls=%async_computation.2 | async-start | bytes 1114112 | tf_op jit(solution)/shard_map/cond/branch_0_fun/all_to_all | solution.py:458
  72.5 14.9 %copy-start.7 = (bf16[1024,512]{1,0:T(8,128)(2,1)S(1)}, bf16[1024,512]{1,0:T(8,128)(2,1)}, u32[]{:S(2)}) copy-start(bf16[1024,512]{1,0:T(8,128)(2,1)} %get-tuple-element.66.pv) | copy-start | bytes 3145732 | tf_op jit(solution)/shard_map/cond

commit v4 on v3

--- a/solution.py
+++ b/solution.py
@@ -285,28 +285,41 @@
     aux = aux[0:8, :] + aux[8:16, :]
     nrm[0:PROMPTS, :] = jnp.concatenate([aux[0:PROMPTS, :], aux[PROMPTS:8, :]], axis=1)
     clane = iota((GROUP, LANES), 1)
+    ones = jnp.ones((2 * LANES, LANES), BF16)
     sums = [jnp.zeros((GROUP, LANES), F32) for _ in range(RLEN // GROUP)]
+
+    def row_sum(x):
+        return dot(jnp.concatenate(split_two(x), axis=1), ones, 1, 0)
+
     for r in range(2):
         norm = jnp.broadcast_to(nrm[pl.ds(rp[2 * me + r, 0], 1), :], (LANES, DK)).astype(BF16)
         state = received(m, r)
         for b in range(RLEN // GROUP):
             rows = slice(b * GROUP, (b + 1) * GROUP)
-            small = cols[rows, :]
-            lifted = small[:, 2 + r : 3 + r]
+            lifted = jnp.broadcast_to(cols[rows, 2 + r : 3 + r], (GROUP, LANES))
+            den = jnp.broadcast_to(cols[rows, r : r + 1], (GROUP, LANES))
             query = q[r, rows, :]
-            den = small[:, r : r + 1] + lifted * dot(query, norm, 1, 1)[:, 0:1]
+            den = den + lifted * dot(query, norm, 1, 1)
             inverse = lax.rsqrt(den * den + 1.0)
-            hidden = (num[r, rows, :].astype(F32) + lifted * dot(query, state, 1, 0)) * inverse
-            hid[r, rows, :] = hidden.astype(BF16)
-            squares = jnp.sum(hidden * hidden, axis=1, keepdims=True)
-            dots = jnp.sum(og[r, rows, :].astype(F32) * gain[...] * hidden, axis=1, keepdims=True)
             lift = lifted * inverse
+            squares = jnp.zeros((GROUP, LANES), F32)
+            dots = jnp.zeros((GROUP, LANES), F32)
+            for c in range(TILES):
+                tile = slice(c * LANES, (c + 1) * LANES)
+                if c % 2 == 0:
+                    pair = slice(c * LANES, (c + 2) * LANES)
+                    both = dot(query, state[:, pair], 1, 0)
+                lifting = both[:, (c % 2) * LANES : (c % 2 + 1) * LANES]
+                hidden = (num[r, rows, tile].astype(F32) + lifted * lifting) * inverse
+                hid[r, rows, tile] = hidden.astype(BF16)
+                squares = squares + hidden * hidden
+                dots = dots + og[r, rows, tile].astype(F32) * gain[:, tile] * hidden
             total = sums[b]
             for at, value in (
-                (2 * r, squares),
-                (2 * r + 1, dots),
-                (4 + r, lift),
-                (6 + r, den * inverse * lift),
+                (2 * r, row_sum(squares)),
+                (2 * r + 1, row_sum(dots)),
+                (16 + 2 * r, lift),
+                (32 + 2 * r, den * inverse * lift),
             ):
                 total = jnp.where(clane == at, value, total)
             sums[b] = total
@@ -320,7 +333,7 @@
         msg[dev] = rows
 
 
-def grad_kernel(m, hid, cols2, og, gain, q, msg, inv_out, numer, denom):
+def grad_kernel(m, hid, cols2, og, gain, q, msg, out_hbm, numer, denom, out, sems):
     total = m[0]
     for dev in range(1, HEADS):
         total = total + m[dev]
@@ -328,57 +341,49 @@
     total = jnp.concatenate([total, jnp.zeros((LANES - 16, LANES), F32)], axis=0).T
     inverses = lax.rsqrt(total / features + 1e-6)
     coefs = pltpu.roll(total, LANES - 1, 1) * (inverses * inverses * inverses) / features
-    inv_out[...] = inverses
+    copies = []
+    for c in range(RLEN // LANES):
+        rows = slice(c * LANES, (c + 1) * LANES)
+        shift = (LANES - 4 * c) % LANES
+        inv = pltpu.roll(inverses, shift, 1) if shift else inverses
+        coef = pltpu.roll(coefs, shift, 1) if shift else coefs
+        squares = cols2[rows, :]
+        dots = pltpu.roll(squares, LANES - 1, 1)
+        lift = pltpu.roll(squares, LANES - 16, 1)
+        ratio = pltpu.roll(squares, LANES - 32, 1)
+        small = -(inv * dots - coef * squares) * ratio
+        lane = iota((LANES, LANES), 1)
+        useful = (lane == 0) | (lane == 2)
+        denom[rows, :] = jnp.where(useful, small, 0.0).astype(BF16)
+        by_grad, by_hidden = inv * lift, coef * lift
+        for r in range(2):
+            at = slice(2 * r, 2 * r + 1)
+            grads = gain[...] * og[r, rows, :].astype(F32)
+            hidden = hid[r, rows, :].astype(F32)
+            numer[r, rows, :] = (grads * by_grad[:, at] - hidden * by_hidden[:, at]).astype(BF16)
+            out[r, rows, :] = (hidden * gain[...] * inv[:, at]).astype(BF16)
+            place = pl.ds(c * LANES, LANES)
+            copies.append(
+                pltpu.make_async_copy(out.at[r, place], out_hbm.at[r, place], sems.at[2 * c + r])
+            )
+            copies[-1].start()
     rows8 = []
     for r in range(2):
-        for c in range(RLEN // LANES):
-            rows = slice(c * LANES, (c + 1) * LANES)
-            at = 4 * c + 2 * r
-            inv, coef = inverses[:, at : at + 1], coefs[:, at : at + 1]
-            small = cols2[rows, :]
-            squares, dots = small[:, 2 * r : 2 * r + 1], small[:, 2 * r + 1 : 2 * r + 2]
-            ratio = small[:, 6 + r : 7 + r]
-            lift = small[:, 4 + r : 5 + r]
-            grads = gain[...] * og[r, rows, :].astype(F32)
-            numer[rows, :] = (grads * (inv * lift) - hid[r, rows, :].astype(F32) * (coef * lift)).astype(BF16)
-            lift_denom = (-(inv * dots - coef * squares) * ratio).astype(BF16).astype(F32)
-            part = jnp.sum(lift_denom * q[r, rows, :].astype(F32), axis=0, keepdims=True)
-            denom[...] = part if c == 0 else denom[...] + part
-        state = dot(q[r], numer[...], 0, 0).astype(BF16)
+        state = dot(q[r], numer[r], 0, 0).astype(BF16)
         for dev in range(SEQ):
             send_state(msg, dev, r, state[dev * ROWS : (dev + 1) * ROWS, :])
-        for piece in split_two(denom[...]):
+        norm = dot(denom[...], q[r], 0, 0)[2 * r : 2 * r + 1, :]
+        for piece in split_two(norm):
             piece = piece.astype(F32)
             rows8 += [piece[:, 0:LANES], piece[:, LANES:DK]]
     aux = jnp.concatenate(rows8, axis=0).astype(BF16)
     for dev in range(SEQ):
         msg[dev, 2 * STATE : 2 * STATE + AUX, :] = aux
-
-
-def out_kernel(len_ref, hid, inverses, gain, expo, aft, pk, out, columns_out, weighted):
-    me = lax.axis_index("seq")
-    groups = WIN // LANES
-    pid = window_pid(me, ends_of(len_ref))
-    after = jnp.zeros((groups, LANES), F32)
-    for p in range(PROMPTS):
-        after = jnp.where(pid == p, aft[0:1, p : p + 1], after)
-    weight = jnp.exp(expo[...] + after)
-    columns = jnp.concatenate(
-        [weight, pid.astype(F32), jnp.zeros((LANES - 2 * groups, LANES), F32)], axis=0
-    ).T
-    columns_out[...] = columns
-    for r in range(groups):
-        rows = slice(r * LANES, (r + 1) * LANES)
-        weighted[rows, :] = (pk[rows, :].astype(F32) * columns[:, r : r + 1]).astype(BF16)
-    for r in range(2):
-        for c in range(RLEN // LANES):
-            rows = slice(c * LANES, (c + 1) * LANES)
-            at = 4 * c + 2 * r
-            inv = inverses[:, at : at + 1]
-            out[r, rows, :] = (hid[r, rows, :].astype(F32) * gain[...] * inv).astype(BF16)
-
-
-def gather_kernel(slots, len_ref, rp, m, unused, out, gn, acc, aacc, low):
+    for copy in copies:
+        copy.wait()
+
+
+def gather_kernel(slots, len_ref, rp, m, out, gn, acc, aacc, low):
     ends = ends_of(len_ref)
     acc[...] = jnp.zeros_like(acc)
     aacc[...] = jnp.zeros_like(aacc)
@@ -402,13 +407,20 @@
 
 
 def prompt_kernel(
-    slots, len_ref, m, gn, columns_ref, weighted_ref, pv, kg_hbm, vg_hbm, kg, vg, sems
+    slots, len_ref, m, gn, expo, aft, pk, pv, kg_hbm, vg_hbm, kg, vg, sems
 ):
     me = lax.axis_index("seq")
     ends = ends_of(len_ref)
     groups = WIN // LANES
     first = first_prompt(me, ends, slots)
-    columns = columns_ref[...]
+    pid = window_pid(me, ends)
+    after = jnp.zeros((groups, LANES), F32)
+    for p in range(PROMPTS):
+        after = jnp.where(pid == p, aft[0:1, p : p + 1], after)
+    weight = jnp.exp(expo[...] + after)
+    columns = jnp.concatenate(
+        [weight, pid.astype(F32), jnp.zeros((LANES - 2 * groups, LANES), F32)], axis=0
+    ).T
 
     def at_row(j):
         total = jnp.int32(0)
@@ -426,7 +438,7 @@
             )
             for at in (0, groups)
         )
-        weighted = weighted_ref[rows, :]
+        weighted = (pk[rows, :].astype(F32) * w).astype(BF16)
         low, high = at_row(g * GROUP), at_row((g + 1) * GROUP - 1)
 
         def grads(p):
@@ -507,24 +519,23 @@
         name="hidden_kernel",
     )(rp, q, got2, num, cols, og, gain)
     got3 = exchange(msg3, "head")
-    msg4, inverses = call(
+    msg4, resp_out = call(
         grad_kernel,
         [VMEM] * 6,
-        [((SEQ, 2 * STATE + AUX, LANES), BF16), ((LANES, LANES), F32)],
-        [pltpu.VMEM((RLEN, DV), BF16), pltpu.VMEM((1, DK), F32)],
+        [((SEQ, 2 * STATE + AUX, LANES), BF16), ((2, RLEN, DV), BF16)],
+        [
+            pltpu.VMEM((2, RLEN, DV), BF16),
+            pltpu.VMEM((RLEN, LANES), BF16),
+            pltpu.VMEM((2, RLEN, DV), BF16),
+            pltpu.SemaphoreType.DMA((2 * RLEN // LANES,)),
+        ],
+        spec=(VMEM, HBM),
         name="grad_kernel",
     )(got3, hid, cols2, og, gain, q)
     got4 = exchange(msg4, "seq")
-    resp_out, columns, weighted = call(
-        out_kernel,
-        [SMEM] + [VMEM] * 6,
-        [((2, RLEN, DV), BF16), ((LANES, LANES), F32), ((WIN, DK), BF16)],
-        [],
-        name="out_kernel",
-    )(lengths, hid, inverses, gain, expo, aft, pk)
     msg5, gn = call(
         part(gather_kernel, slots),
-        [SMEM, SMEM, VMEM, ANY],
+        [SMEM, SMEM, VMEM],
         [((SEQ, slots * STATE, LANES), BF16), ((8, DK), F32)],
         [
             pltpu.VMEM((PROMPTS, STATE, LANES), F32),
@@ -532,11 +543,11 @@
             pltpu.VMEM((PROMPTS, STATE, LANES), BF16),
         ],
         name="gather_kernel",
-    )(lengths, rp, got4, columns)
+    )(lengths, rp, got4)
     got5 = exchange(msg5, "seq")
     key_grad, value_grad = call(
         part(prompt_kernel, slots),
-        [SMEM] + [VMEM] * 5,
+        [SMEM] + [VMEM] * 6,
         [((WIN, DK), BF16), ((WIN, DV), BF16)],
         [
             pltpu.VMEM((WIN, DK), BF16),
@@ -545,7 +556,7 @@
         ],
         spec=HBM,
         name="prompt_kernel",
-    )(lengths, got5, gn, columns, weighted, pv)
+    )(lengths, got5, gn, expo, aft, pk, pv)
     return resp_out, key_grad, value_grad
 
 

time: 90.9 us -> 89 us (0.979)
  blocking collectives: 38.1 us -> 52.8 us
  waiting for transfers between devices: 17.1 us -> 7.24 us
  starting transfers between devices: 11.6 us -> 8.05 us
  Pallas kernels: 21.5 us -> 18.4 us
    all_to_all x3 -> x4, blocking collectives: 38.1 us -> 52.8 us  [exchange(): return lax.all_to_all(x, axis, 0, 0, tiled=True)]
    all_to_all x2 -> x1, waiting for transfers between devices: 17.1 us -> 7.24 us  [exchange(): return lax.all_to_all(x, axis, 0, 0, tiled=True)]
    all_to_all x2 -> x1, starting transfers between devices: 11.6 us -> 8.05 us  [exchange(): return lax.all_to_all(x, axis, 0, 0, tiled=True)]
    pallas_call x4 -> x3, Pallas kernels: 8.79 us -> 6.79 us  [the longest x1 3.3 us: rest(): call(part(prompt_kernel, slots), [SMEM] + [VMEM] * 6, [((WIN, DK), BF16),...]
    pallas_call x1, Pallas kernels: 3.51 us -> 2.52 us  [rest(): call(hidden_kernel, [SMEM] + [VMEM] * 6, [((2, RLEN, DV), BF16), ((RLEN,...]
  transfers between devices with their start and end apart: 2 -> 1, of which waited for: 2 -> 1; matrix products, arithmetic and copies ran while one was open for 0% -> 0% of each run, Pallas kernels for 7% -> 4%
where the time goes in v4:
time: 89 us; the launch traced here: 88.7 us
  blocking collectives  52.8 us (59%)
  Pallas kernels  18.4 us (21%)
  starting transfers between devices  8.05 us (9%)
  waiting for transfers between devices  7.24 us (8%)
  between operations  1.74 us (2%)
    all_to_all x4, blocking collectives, exchange(): return lax.all_to_all(x, axis, 0, 0, tiled=True)  52.8 us
    all_to_all x1, starting transfers between devices, exchange(): return lax.all_to_all(x, axis, 0, 0, tiled=True)  8.05 us
    all_to_all x1, waiting for transfers between devices, exchange(): return lax.all_to_all(x, axis, 0, 0, tiled=True)  7.24 us
    pallas_call x1, Pallas kernels, local(): call(respond_kernel, [VMEM] * 5, [((2, RLEN, DV), BF16), ((RLEN, LANES),...  3.78 us
    pallas_call x1, Pallas kernels, states(): call(functools.partial(state_kernel, slots), [HBM] * 5, [((SEQ, slots * S...  3.49 us
    pallas_call x1, Pallas kernels, rest(): call(part(prompt_kernel, slots), [SMEM] + [VMEM] * 6, [((WIN, DK), BF16),...  3.3 us
    pallas_call x1, Pallas kernels, rest(): call(hidden_kernel, [SMEM] + [VMEM] * 6, [((2, RLEN, DV), BF16), ((RLEN,...  2.52 us
    pallas_call x1, Pallas kernels, rest(): call(grad_kernel, [VMEM] * 6, [((SEQ, 2 * STATE + AUX, LANES), BF16), ((2...  2.42 us
  transfers between devices with their start and end apart: 1, of which 1 were waited for; matrix products, arithmetic and copies ran while one was open for 0% of the time, Pallas kernels for 4%

profile of v4, /device:TPU:0, one launch (start us, length us, event | category | flops | bytes accessed | tf_op | source)
XLA Modules:
  0.0 88.7 jit_solution(18012660428072883089)
XLA Ops:
  0.6 0.0 copy-start.3
  0.6 0.0 copy-start.2
  0.7 0.0 copy-start
  0.7 0.0 copy-start.1
  0.7 3.5 %state_kernel.3 = (bf16[16,136,128]{2,1,0:T(8,128)(2,1)}, f32[8,128]{1,0:T(8,128)S(1)}, s32[1]{0:T(128)}) custom-call(s32[4]{0:T(128)} %len_hbm.1, bf16[1024,256]{1,0:T(8,128)(2,1)} %pk_hbm.1, bf16[1024,512]{1,0:T(8,128)(2,1)} %pv_hbm.1, f32[1,1024]{1,0:T(1,128)} %pin_hbm.1, f32[1,1024]{1,0:T(1,128)} %pf_hbm.1), custom_call_target="tpu_custom_call" | custom-call | tf_op jit(solution)/shard_map/state_kernel/pallas_call | solution.py:475
  4.2 8.0 %all-to-all-start.9 = ((bf16[16,136,128]{2,1,0:T(8,128)(2,1)}), bf16[16,136,128]{2,1,0:T(8,128)(2,1)}, u32[]{:S(2)}, u32[]{:S(2)}) async-start(bf16[16,136,128]{2,1,0:T(8,128)(2,1)} %get-tuple-element.99), calls=%async_computation.9 | async-start | bytes 1114112 | tf_op jit(solution)/shard_map/all_to_all | solution.py:470
  12.2 0.0 copy-start.4
  12.2 0.0 copy-start.5
  12.2 0.0 copy-start.12
  12.3 0.0 copy-start.13
  12.3 0.0 copy-start.14
  12.3 0.0 copy-start.15
  12.3 0.0 copy-start.16
  13.1 0.0 copy-done.3
  13.1 0.0 copy-done.2
  13.1 0.0 copy-done
  13.1 0.0 copy-done.1
  13.1 3.8 %respond_kernel.1 = (bf16[2,512,512]{2,1,0:T(8,128)(2,1)}, f32[512,128]{1,0:T(8,128)S(1)}) custom-call(bf16[2,512,256]{2,1,0:T(8,128)(2,1)} %q.1, bf16[2,512,256]{2,1,0:T(8,128)(2,1)S(1)} %copy-done.1, bf16[2,512,512]{2,1,0:T(8,128)(2,1)S(1)} %copy-done, f32[1,2,512]{2,1,0:T(2,128)S(1)} %copy-done.2, f32[1,2,512]{2,1,0:T(2,128)S(1)} %copy-done.3), custom_call_target="tpu_custom_call" | custom-call | tf_op jit(solution)/shard_map/respond_kernel/pallas_call | solution.py:566
  16.9 7.2 %all-to-all-done.9 = bf16[16,136,128]{2,1,0:T(8,128)(2,1)} async-done(((bf16[16,136,128]{2,1,0:T(8,128)(2,1)}), bf16[16,136,128]{2,1,0:T(8,128)(2,1)}, u32[]{:S(2)}, u32[]{:S(2)}) %all-to-all-start.9) | async-done | bytes 557088 | tf_op jit(solution)/shard_map/all_to_all | solution.py:470
  24.1 0.0 copy-done.4
  24.1 0.0 copy-done.5
  24.1 0.0 copy-done.12
  24.1 0.0 copy-done.13
  24.1 0.0 copy-done.14
  24.2 0.0 copy-done.15
  24.2 0.0 copy-done.16
  24.2 64.3 %conditional.1 = (bf16[2,512,512]{2,1,0:T(8,128)(2,1)}, bf16[1024,256]{1,0:T(8,128)(2,1)}, bf16[1024,512]{1,0:T(8,128)(2,1)}) conditional(s32[]{:T(128)} %bitcast, (s32[4]{0:T(128)S(1)}, s32[32,1]{0,1:T(1,128)S(1)}, bf16[16,136,128]{2,1,0:T(8,128)(2,1)}, f32[8,128]{1,0:T(8,128)S(1)}, bf16[1024,256]{1,0:T(8,128)(2,1)S(1)}, ...), branch_computations={%region_0.0_spmd, %region_1.0_spmd} | conditional | bytes 18252172 | solution.py:574
  24.2 0.1 copy.16.rp
  24.3 0.0 copy-start.8
  24.3 0.0 copy-start.10
  24.3 1.9 %spread_kernel.2 = (bf16[16,144,128]{2,1,0:T(8,128)(2,1)S(1)}, f32[8,128]{1,0:T(8,128)S(1)}) custom-call(s32[4]{0:T(128)S(1)} %get-tuple-element.46.len_ref, s32[32,1]{1,0:T(8,128)S(1)} %copy.16.rp, bf16[16,136,128]{2,1,0:T(8,128)(2,1)} %get-tuple-element.47.m, f32[8,128]{1,0:T(8,128)S(1)} %get-tuple-element.48.expo, ...), custom_call_target="tpu_custom_call" | custom-call | tf_op jit(solution)/shard_map/cond/branch_0_fun/spread_kernel/pallas_call | solution.py:502
  26.2 14.4 %all_to_all.41.m = bf16[16,144,128]{2,1,0:T(8,128)(2,1)S(1)} all-to-all(bf16[16,144,128]{2,1,0:T(8,128)(2,1)S(1)} %get-tuple-element.51), channel_id=1, replica_groups=mesh['seq'=16,'head'=8] {'seq'}, dimensions={0} | all-to-all | bytes 1179648 | tf_op jit(solution)/shard_map/cond/branch_0_fun/all_to_all | solution.py:470
  40.5 0.0 copy-done.8
  40.5 0.0 copy-done.10
  40.5 2.5 %hidden_kernel.2 = (bf16[2,512,512]{2,1,0:T(8,128)(2,1)S(1)}, f32[512,128]{1,0:T(8,128)S(1)}, f32[8,16,128]{2,1,0:T(8,128)S(1)}) custom-call(s32[32,1]{1,0:T(8,128)S(1)} %copy.16.rp, bf16[2,512,256]{2,1,0:T(8,128)(2,1)S(1)} %copy-done.8, bf16[16,144,128]{2,1,0:T(8,128)(2,1)S(1)} %all_to_all.41.m, bf16[2,512,512]{2,1,0:T(8,128)(2,1)S(1)} %copy-done.10, ...), custom_call_target="tpu_custom_call" | custom-call | tf_op jit(solution)/shard_map/cond/branch_0_fun/hidden_kernel/pallas_call | solution.py:514
  43.1 9.9 %all_to_all.42.m = f32[8,16,128]{2,1,0:T(8,128)S(1)} all-to-all(f32[8,16,128]{2,1,0:T(8,128)S(1)} %get-tuple-element.55), channel_id=1, replica_groups=mesh['seq'=16,'head'=8] {'head'}, dimensions={0} | all-to-all | bytes 131072 | tf_op jit(solution)/shard_map/cond/branch_0_fun/all_to_all | solution.py:470
  52.9 2.4 %grad_kernel.2 = (bf16[16,136,128]{2,1,0:T(8,128)(2,1)S(1)}, bf16[2,512,512]{2,1,0:T(8,128)(2,1)}) custom-call(f32[8,16,128]{2,1,0:T(8,128)S(1)} %all_to_all.42.m, bf16[2,512,512]{2,1,0:T(8,128)(2,1)S(1)} %get-tuple-element.56.hid, f32[512,128]{1,0:T(8,128)S(1)} %get-tuple-element.57.cols2, bf16[2,512,512]{2,1,0:T(8,128)(2,1)S(1)} %get-tuple-element.53.og, ...), custom_call_target="tpu_custom_call" | custom-call | tf_op jit(solution)/shard_map/cond/branch_0_fun/grad_kernel/pallas_call | solution.py:522
  55.4 15.1 %all_to_all.43.m = bf16[16,136,128]{2,1,0:T(8,128)(2,1)S(1)} all-to-all(bf16[16,136,128]{2,1,0:T(8,128)(2,1)S(1)} %get-tuple-element.59), channel_id=1, replica_groups=mesh['seq'=16,'head'=8] {'seq'}, dimensions={0} | all-to-all | bytes 1114112 | tf_op jit(solution)/shard_map/cond/branch_0_fun/all_to_all | solution.py:470
  70.5 0.0 copy-start.6
  70.5 1.1 %gather_kernel.2 = (bf16[16,128,128]{2,1,0:T(8,128)(2,1)S(1)}, f32[8,256]{1,0:T(8,128)S(1)}) custom-call(s32[4]{0:T(128)S(1)} %get-tuple-element.46.len_ref, s32[32,1]{1,0:T(8,128)S(1)} %copy.16.rp, bf16[16,136,128]{2,1,0:T(8,128)(2,1)S(1)} %all_to_all.43.m), custom_call_target="tpu_custom_call" | custom-call | tf_op jit(solution)/shard_map/cond/branch_0_fun/gather_kernel/pallas_call | solution.py:536
  71.6 13.4 %all_to_all.44.m = bf16[16,128,128]{2,1,0:T(8,128)(2,1)S(1)} all-to-all(bf16[16,128,128]{2,1,0:T(8,128)(2,1)S(1)} %get-tuple-element.60), channel_id=1, replica_groups=mesh['seq'=16,'head'=8] {'seq'}, dimensions={0} | all-to-all | bytes 1048576 | tf_op jit(solution)/shard_map/cond/branch_0_fun/all_to_all | solution.py:470
  85.0 0.0 copy-done.6
  85.0 3.3 %prompt_kernel.2 = (bf16[1024,256]{1,0:T(8,128)(2,1)}, bf16[1024,512]{1,0:T(8,128)(2,1)}) custom-call(s32[4]{0:T(128)S(1)} %get-tuple-element.46.len_ref, bf16[16,128,128]{2,1,0:T(8,128)(2,1)S(1)} %all_to_all.44.m, f32[8,256]{1,0:T(8,128)S(1)} %get-tuple-element.61.gn, f32[8,128]{1,0:T(8,128)S(1)} %get-tuple-element.48.expo, ...), custom_call_target="tpu_custom_call" | custom-call | tf_op jit(solution)/shard_map/cond/branch_0_fun/prompt_kernel/pallas_call | solution.py:548
Async XLA Ops:
  0.6 12.4 %copy-start.3 = (f32[1,2,512]{2,1,0:T(2,128)S(1)}, f32[1,2,512]{2,1,0:T(2,128)}, u32[]{:S(2)}) copy-start(f32[1,2,512]{2,1,0:T(2,128)} %rf.1) | copy-start | bytes 12292
  0.6 12.4 %copy-start.2 = (f32[1,2,512]{2,1,0:T(2,128)S(1)}, f32[1,2,512]{2,1,0:T(2,128)}, u32[]{:S(2)}) copy-start(f32[1,2,512]{2,1,0:T(2,128)} %rin.1) | copy-start | bytes 12292
  0.7 12.4 %copy-start = (bf16[2,512,512]{2,1,0:T(8,128)(2,1)S(1)}, bf16[2,512,512]{2,1,0:T(8,128)(2,1)}, u32[]{:S(2)}) copy-start(bf16[2,512,512]{2,1,0:T(8,128)(2,1)} %v.1) | copy-start | bytes 3145732
  0.7 12.4 %copy-start.1 = (bf16[2,512,256]{2,1,0:T(8,128)(2,1)S(1)}, bf16[2,512,256]{2,1,0:T(8,128)(2,1)}, u32[]{:S(2)}) copy-start(bf16[2,512,256]{2,1,0:T(8,128)(2,1)} %k.1) | copy-start | bytes 1572868
  4.2 20.0 %all-to-all-start.9 = ((bf16[16,136,128]{2,1,0:T(8,128)(2,1)}), bf16[16,136,128]{2,1,0:T(8,128)(2,1)}, u32[]{:S(2)}, u32[]{:S(2)}) async-start(bf16[16,136,128]{2,1,0:T(8,128)(2,1)} %get-tuple-element.99), calls=%async_computation.9 | async-start | bytes 1114112 | tf_op jit(solution)/shard_map/all_to_all | solution.py:470
  12.2 11.9 %copy-start.4 = (bf16[1024,256]{1,0:T(8,128)(2,1)S(1)}, bf16[1024,256]{1,0:T(8,128)(2,1)}, u32[]{:S(2)}) copy-start(bf16[1024,256]{1,0:T(8,128)(2,1)} %pk_hbm.1) | copy-start | bytes 1572868
  12.2 11.9 %copy-start.5 = (bf16[2,512,512]{2,1,0:T(8,128)(2,1)S(1)}, bf16[2,512,512]{2,1,0:T(8,128)(2,1)}, u32[]{:S(2)}) copy-start(bf16[2,512,512]{2,1,0:T(8,128)(2,1)} %param.27) | copy-start | bytes 3145732
  12.2 11.9 %copy-start.12 = (f32[512]{0:T(512)S(1)}, f32[512]{0:T(512)}, u32[]{:S(2)}) copy-start(f32[512]{0:T(512)} %param.26) | copy-start | bytes 6148
  12.3 11.9 %copy-start.13 = (s32[4]{0:T(128)S(1)}, s32[4]{0:T(128)}, u32[]{:S(2)}) copy-start(s32[4]{0:T(128)} %len_hbm.1) | copy-start | bytes 52
  12.3 11.9 %copy-start.14 = (f32[1,1024]{1,0:T(1,128)S(1)}, f32[1,1024]{1,0:T(1,128)}, u32[]{:S(2)}) copy-start(f32[1,1024]{1,0:T(1,128)} %pin_hbm.1) | copy-start | bytes 12292
  12.3 11.9 %copy-start.15 = (f32[1,1024]{1,0:T(1,128)S(1)}, f32[1,1024]{1,0:T(1,128)}, u32[]{:S(2)}) copy-start(f32[1,1024]{1,0:T(1,128)} %pf_hbm.1) | copy-start | bytes 12292
  12.3 11.9 %copy-start.16 = (s32[32,1]{0,1:T(1,128)S(1)}, s32[32,1]{0,1:T(1,128)}, u32[]{:S(2)}) copy-start(s32[32,1]{0,1:T(1,128)} %param.20) | copy-start | bytes 388
  24.3 16.3 %copy-start.8 = (bf16[2,512,256]{2,1,0:T(8,128)(2,1)S(1)}, bf16[2,512,256]{2,1,0:T(8,128)(2,1)}, u32[]{:S(2)}) copy-start(bf16[2,512,256]{2,1,0:T(8,128)(2,1)} %get-tuple-element.45.q) | copy-start | bytes 1572868 | tf_op jit(solution)/shard_map/cond
  24.3 16.3 %copy-start.10 = (bf16[2,512,512]{2,1,0:T(8,128)(2,1)S(1)}, bf16[2,512,512]{2,1,0:T(8,128)(2,1)}, u32[]{:S(2)}) copy-start(bf16[2,512,512]{2,1,0:T(8,128)(2,1)} %get-tuple-element.52.num) | copy-start | bytes 3145732 | tf_op jit(solution)/shard_map/cond
  70.5 14.5 %copy-start.6 = (bf16[1024,512]{1,0:T(8,128)(2,1)S(1)}, bf16[1024,512]{1,0:T(8,128)(2,1)}, u32[]{:S(2)}) copy-start(bf16[1024,512]{1,0:T(8,128)(2,1)} %get-tuple-element.63.pv) | copy-start | bytes 3145732 | tf_op jit(solution)/shard_map/cond
